TPU v7x, 256 devices: a whole 4x4x8 slice. The times are simulated.
256 devices in a mesh: group: 4 (over x), dp: 64 (over y, z, core).
Axes of the slice: x: 4, y: 4, z: 8, core: 2. Of those that a mesh axis runs over, the one named last changes fastest.
Arguments:
- hidden: bfloat16 [65536, 2048], P(('group', 'dp')), may hold values from 0 to 40, as said below
- weight: bfloat16 [2048, 1024], replicated, may hold values from -0.125 to 0.125
- partners: int32 [256, 256], P(('group', 'dp')), may hold values from 0 to 255, each once within a row
Outputs:
- whitened: bfloat16 [65536, 1024], P(('group', 'dp'))
- grad_weight: float32 [2048, 1024], P(('group', 'dp'))
- grad_hidden: bfloat16 [65536, 2048], P(('group', 'dp'))
Inputs may be any that keep to these rules, and one draw needn't show every extreme that they name: `hidden`: nonnegative activations. `partners`: each row is a permutation of 0 to 255.
All inputs are finite; a program needn't handle non-finite values.
Results may differ from a plain program's by a relative error of at most 0.0089.
Values sent between devices are 32-bit elements; how exact they have to be, the bound alone decides.
A program may use at most 128 MiB of HBM per device.

v0:
```python
import jax
import jax.numpy as jnp
from jax import lax
from jax.sharding import PartitionSpec as P

epsilon = 1e-06
highest = lax.Precision.HIGHEST


def body(hidden, weight, partners):
    local_rows = hidden.shape[0]
    total_rows = local_rows * lax.axis_size("group") * lax.axis_size("dp")
    embedded = jnp.dot(hidden, weight, preferred_element_type=jnp.float32)
    mean_row = lax.psum(jnp.sum(embedded, axis=0), ("group", "dp")) / total_rows
    centered = embedded - mean_row
    scatter = lax.psum(jnp.dot(centered.T, centered, precision=highest), ("group", "dp"))
    cov = scatter / (total_rows - 1)
    factor = jnp.linalg.cholesky(cov)
    white = lax.linalg.triangular_solve(
        factor, centered, left_side=False, lower=True, transpose_a=True
    )
    whitened = white.astype(jnp.bfloat16)
    row_norm = jnp.sqrt(jnp.sum(white * white, axis=1, keepdims=True) + epsilon)
    unit = white / row_norm
    partner = partners[0]
    row_ids = jnp.arange(local_rows, dtype=jnp.int32)
    inverse = jnp.zeros((local_rows,), jnp.int32).at[partner].set(row_ids)
    grad_unit = 2.0 * (
        2.0 * unit - jnp.take(unit, partner, axis=0) - jnp.take(unit, inverse, axis=0)
    )
    inner_prod = jnp.sum(white * grad_unit, axis=1, keepdims=True)
    grad_white = grad_unit / row_norm - white * (inner_prod / row_norm**3)
    local_pair = jnp.dot(grad_white.T, white, precision=highest)
    direct = lax.linalg.triangular_solve(
        factor, grad_white, left_side=False, lower=True, transpose_a=False
    )
    pair_moment = lax.psum(local_pair, ("group", "dp"))
    lower_half = -(jnp.tril(pair_moment) - 0.5 * jnp.diag(jnp.diag(pair_moment)))
    left_solved = lax.linalg.triangular_solve(
        factor, lower_half, left_side=True, lower=True, transpose_a=True
    )
    solved = lax.linalg.triangular_solve(
        factor, left_solved, left_side=False, lower=True, transpose_a=False
    )
    grad_cov = 0.5 * (solved + solved.T)
    grad_cent = direct + 2.0 / (total_rows - 1) * jnp.dot(centered, grad_cov, precision=highest)
    column_sums = lax.psum(jnp.sum(grad_cent, axis=0), ("group", "dp"))
    grad_z = (grad_cent - column_sums / total_rows).astype(jnp.bfloat16)
    grad_hidden = jnp.dot(grad_z, weight.T, preferred_element_type=jnp.float32).astype(jnp.bfloat16)
    grad_weight = lax.psum_scatter(
        lax.dot_general(
            hidden, grad_z, (((0,), (0,)), ((), ())), preferred_element_type=jnp.float32
        ),
        ("group", "dp"),
        scatter_dimension=0,
        tiled=True,
    )
    return (whitened, grad_weight, grad_hidden)


def solution(mesh):
    return jax.shard_map(
        body,
        mesh=mesh,
        in_specs=(P(("group", "dp"), None), P(), P(("group", "dp"), None)),
        out_specs=(P(("group", "dp"), None), P(("group", "dp"), None), P(("group", "dp"), None)),
        check_vma=False,
    )
```

profile of v0, /device:TPU:0, one launch (start us, length us, event | category | flops | bytes accessed | tf_op | source)
XLA Modules:
  0.0 2474.8 jit_solution(2633390698742377143)
XLA Ops:
  8.4 3.4 fusion.192
  11.8 79.1 %psum.28 = f32[1024]{0:T(1024)S(1)} all-reduce(f32[1024]{0:T(1024)S(1)} %get-tuple-element.80), channel_id=1, replica_groups=mesh['group'=4,'dp'=64] {'group','dp'}, use_global_device_ids=true, to_apply=%region_1.0 | all-reduce | flops 1024 | bytes 8192 | tf_op jit(solution)/shard_map/psum | solution.py:14
  91.2 5.2 fusion.194
  97.9 261.9 %all-reduce.4.cloned.1.call-done = f32[1024,1024]{0,1:T(8,128)} async-done(((f32[1024,1024]{0,1:T(8,128)}), f32[1024,1024]{0,1:T(8,128)}) %all-reduce.4.cloned.1.call-update) | async-done | bytes 4194320 | tf_op jit(solution)/shard_map/psum | solution.py:16
  359.9 5.1 broadcast_multiply_fusion
  364.9 5.8 copy.27
  370.8 4.5 fusion.3
  377.2 11.7 cholesky.223
  388.9 9.8 custom-call.68
  398.8 2.5 cholesky.255
  401.3 2.4 constant_dynamic-update-slice_fusion.107
  405.2 11.8 cholesky.244
  417.7 9.8 custom-call.69
  428.8 2.1 convolution_subtract_fusion.11
  430.9 11.7 cholesky.468
  443.8 9.8 custom-call.70
  454.8 2.4 convolution_subtract_fusion.12
  457.2 11.9 cholesky.487
  470.4 9.8 custom-call.71
  481.3 2.3 convolution_subtract_fusion.13
  483.7 11.7 cholesky.506
  496.7 10.2 custom-call.72
  507.9 2.3 convolution_subtract_fusion.14
  510.2 11.7 cholesky.526
  523.2 9.8 custom-call.73
  534.0 2.0 convolution_subtract_fusion.27
  536.0 11.8 cholesky.546
  549.1 9.8 custom-call.74
  561.5 11.7 cholesky.564
  580.2 4.8 select_select_fusion
  585.0 27.9 %while.1 = (s32[]{:T(128)}, f32[1024,1024]{1,0:T(8,128)}, s32[8,2]{0,1:T(2,128)S(1)}, f32[8,128,128]{2,1,0:T(8,128)}, s32[]{:T(128)}) while((s32[]{:T(128)}, f32[1024,1024]{1,0:T(8,128)}, s32[8,2]{0,1:T(2,128)S(1)}, f32[8,128,128]{2,1,0:T(8,128)}, s32[]{:T(128)}) %tuple.79), condition=%wide.while_cond, body=%wide.while_body.sunk | while | flops 2 | bytes 132205 | solution.py:19
  585.6 2.9 bitcast_dynamic-update-slice_fusion.2
  589.1 2.9 bitcast_dynamic-update-slice_fusion.2
  592.6 2.9 bitcast_dynamic-update-slice_fusion.2
  596.1 2.9 bitcast_dynamic-update-slice_fusion.2
  599.5 2.9 bitcast_dynamic-update-slice_fusion.2
  603.0 2.9 bitcast_dynamic-update-slice_fusion.2
  606.5 2.9 bitcast_dynamic-update-slice_fusion.2
  610.0 2.8 bitcast_dynamic-update-slice_fusion.2
  612.9 80.2 %custom-call.75 = f32[8,128,128]{1,2,0:T(8,128)} custom-call(f32[8,128,128]{2,1,0:T(8,128)} %get-tuple-element.11), custom_call_target="InvertDiagBlocksLowerTriangular" | custom-call | tf_op jit(solution)/shard_map/triangular_solve | solution.py:19
  703.8 2.2 convolution_subtract_fusion.19
  706.4 2.4 convolution_subtract_fusion.25
  709.1 2.7 convolution_subtract_fusion.29
  714.9 2.0 gather_fusion.2
  717.0 2.0 gather_fusion.1
  720.5 2.5 copy.31
  724.7 2.4 multiply_subtract_fusion
  728.4 5.5 fusion.195
  752.8 259.3 %all-reduce.6.cloned.1.call-done = f32[1024,1024]{1,0:T(8,128)} async-done(((f32[1024,1024]{1,0:T(8,128)}), f32[1024,1024]{1,0:T(8,128)}) %all-reduce.6.cloned.1.call-update) | async-done | bytes 4194320 | tf_op jit(solution)/shard_map/psum | solution.py:37
  1012.1 17.3 gather_fusion
  1029.5 3.0 subtract_negate_fusion
  1044.9 2.5 convolution_subtract_fusion.8
  1053.1 2.7 fusion.39
  1056.4 3.8 fusion.45
  1061.1 4.3 convolution_subtract_fusion.4
  1066.3 5.2 convolution_subtract_fusion.2
  1072.5 5.9 convolution_subtract_fusion.6
  1085.7 5.4 copy.39
  1091.2 10.0 fusion.193
  1101.2 76.2 %psum.31 = f32[1024]{0:T(1024)S(1)} all-reduce(f32[1024]{0:T(1024)S(1)} %get-tuple-element.106), channel_id=1, replica_groups=mesh['group'=4,'dp'=64] {'group','dp'}, use_global_device_ids=true, to_apply=%region_24.26 | all-reduce | flops 1024 | bytes 8192 | tf_op jit(solution)/shard_map/psum | solution.py:47
  1177.4 4.5 convolution_bitcast_fusion
  1181.9 9.3 copy.52
  1193.2 4.7 convolution_convert_fusion
  1197.9 1270.1 %reduce-scatter.4.cloned.1.call-done = f32[8,1024]{1,0:T(8,128)} async-done(((f32[2048,1024]{1,0:T(8,128)}), f32[8,1024]{1,0:T(8,128)}) %reduce-scatter.4.cloned.1.call-update) | async-done | bytes 32784
  (211 shorter events, 96.0 us)
Async XLA Ops:
  7.2 1.2 copy-start
  7.2 352.7 %all-reduce.4.cloned.1.call-start = ((), (), s32[]{:S(2)}) async-start(), calls=%async_computation.1 | async-start | bytes 8388608 | tf_op jit(solution)/shard_map/psum | solution.py:16
  91.1 618.0 %copy-start.2 = (f32[256,1024]{1,0:T(8,128)}, f32[256,1024]{1,0:T(8,128)S(1)}, u32[]{:S(2)}) copy-start(f32[256,1024]{1,0:T(8,128)S(1)} %broadcast_subtract_fusion) | copy-start | bytes 3145732
  91.2 5.3 copy-start.9
  96.4 915.7 %all-reduce.6.cloned.1.call-start = ((), (), s32[]{:S(2)}) async-start(), calls=%async_computation.2 | async-start | bytes 8388608 | tf_op jit(solution)/shard_map/psum | solution.py:37
  375.3 1.9 copy-start.4
  693.1 8.1 copy-start.6
  727.1 1.3 copy-start.5
  727.1 8.0 copy-start.7
  744.8 1723.3 %reduce-scatter.4.cloned.1.call-start = ((), (), s32[]{:S(2)}) async-start(), calls=%async_computation.3 | async-start | bytes 8421376
  1029.4 3.6 copy-start.1
  1085.7 5.4 copy-start.3
  1191.2 1.0 copy-start.8
Sparse Core Ops, SparseCore 0:
  96.5 263.3 all-reduce.3
  744.9 267.1 all-reduce.5
  1191.3 1276.6 reduce-scatter.3
where the time goes:
time: 2480 us; the launch traced here: 2470 us
  waiting for transfers between devices  1790 us (72%)
  other arithmetic  275 us (11%)
  blocking collectives  155 us (6%)
  matrix products  136 us (5%)
  local copies, waits for them, and re-layouts  96.8 us (4%)
    unnamed x4, waiting for transfers between devices  1270 us
    psum x1, waiting for transfers between devices, body(): lax.psum(jnp.dot(centered.T, centered, precision=highest), ('group', 'dp'))  262 us
    psum x1, waiting for transfers between devices, body(): pair_moment = lax.psum(local_pair, ('group', 'dp'))  259 us
    another operation x30, other arithmetic, body(): factor = jnp.linalg.cholesky(cov)  172 us
    another operation x3, other arithmetic, body(): lax.linalg.triangular_solve(factor, centered, left_side=False, lower=True...  85 us
    psum x1, blocking collectives, body(): mean_row = lax.psum(jnp.sum(embedded, axis=0), ('group', 'dp')) / total_rows  79.1 us
    psum x1, blocking collectives, body(): column_sums = lax.psum(jnp.sum(grad_cent, axis=0), ('group', 'dp'))  76.2 us
  transfers between devices with their start and end apart: 3, of which 3 were waited for; matrix products, arithmetic and copies ran while one was open for 1% of the time, Pallas kernels for 0%

commit v1 on v0

v1 whole, which is shorter than its diff:
```python
import jax
import jax.numpy as jnp
from jax import lax
from jax.experimental import pallas as pl
from jax.experimental.pallas import tpu as pltpu
from jax.sharding import PartitionSpec as P

epsilon = 1e-06
highest = lax.Precision.HIGHEST
MESH = pl.DeviceIdType.MESH
NX, NY, NZ, NC = 4, 4, 8, 2
BLK = 128
MB = 1 << 20


def place():
    dp = lax.axis_index("dp")
    x = lax.axis_index("group")
    return x, lax.div(dp, NZ * NC), lax.rem(lax.div(dp, NC), NZ), lax.rem(dp, NC)


def device(x, y, z, c):
    return (x, (y * NZ + z) * NC + c)


def x_peers(x, y, z, c):
    return [device(lax.rem(x + k, NX), y, z, c) for k in range(1, NX)]


def y_peers(x, y, z, c):
    return [device(x, lax.rem(y + k, NY), z, c) for k in range(1, NY)]


def z_peers(x, y, z, c):
    return [device(x, y, lax.rem(z + k, NZ), c) for k in range(1, NZ)]


def meet(peers):
    barrier = pltpu.get_barrier_semaphore()
    for peer in peers:
        pl.semaphore_signal(barrier, inc=1, device_id=peer, device_id_type=MESH)
    pl.semaphore_wait(barrier, len(peers))


def send(src, dst, sems, slot, peer):
    copy = pltpu.make_async_remote_copy(
        src_ref=src,
        dst_ref=dst,
        send_sem=sems.at[0, slot],
        recv_sem=sems.at[1, slot],
        device_id=peer,
        device_id_type=MESH,
    )
    copy.start()
    return copy


def tile_sum_kernel(in_ref, out_ref, part, got_a, got_b, sems):
    x, y, z, c = place()
    near = []
    for k in range(1, NZ * NC):
        own = lax.rem(z * NC + c + k, NZ * NC)
        near.append(device(x, y, lax.div(own, NC), lax.rem(own, NC)))
    far = []
    for k in range(1, NX * NY):
        own = lax.rem(x * NY + y + k, NX * NY)
        far.append(device(lax.div(own, NY), lax.rem(own, NY), z, c))
    meet(near + far)
    copies = [send(in_ref, got_a.at[k], sems, k, peer) for k, peer in enumerate(near)]
    total = in_ref[...]
    for k, copy in enumerate(copies):
        copy.wait()
        total = total + got_a[k]
    part[...] = total
    copies = [send(part, got_b.at[k], sems, 15 + k, peer) for k, peer in enumerate(far)]
    for k, copy in enumerate(copies):
        copy.wait()
        total = total + got_b[k]
    out_ref[...] = total


def tile_sum(tile, collective_id):
    vmem = pl.BlockSpec(memory_space=pltpu.VMEM)
    return pl.pallas_call(
        tile_sum_kernel,
        out_shape=jax.ShapeDtypeStruct((8, 128), jnp.float32),
        in_specs=[vmem],
        out_specs=vmem,
        scratch_shapes=[
            pltpu.VMEM((8, 128), jnp.float32),
            pltpu.VMEM((15, 8, 128), jnp.float32),
            pltpu.VMEM((15, 8, 128), jnp.float32),
            pltpu.SemaphoreType.DMA((2, 30)),
        ],
        compiler_params=pltpu.CompilerParams(collective_id=collective_id, has_side_effects=True),
        name="tile_sum",
    )(tile)


TILES = 9


def all_sum_kernel(in_ref, out_ref, acc, got_c, got_1, acc_1, got_2, acc_2, got_z, full_z, sems):
    x, y, z, c = place()
    here = (x, y, z, c)
    across = device(x, y, z, 1 - c)
    xs, ys, zs = x_peers(*here), y_peers(*here), z_peers(*here)
    meet([across] + xs + ys + zs)
    copy = send(in_ref.at[1 - c], got_c, sems, 0, across)
    copy.wait()
    acc[...] = in_ref[c] + got_c[...]
    copies = []
    for k in range(3):
        copies.append(send(acc.at[0, lax.rem(x + k + 1, NX)], got_1.at[0, k], sems, 1 + k, xs[k]))
        copies.append(send(acc.at[1, lax.rem(y + k + 1, NY)], got_1.at[1, k], sems, 4 + k, ys[k]))
    for copy in copies:
        copy.wait()
    acc_1[0] = acc[0, x] + got_1[0, 0] + got_1[0, 1] + got_1[0, 2]
    acc_1[1] = acc[1, y] + got_1[1, 0] + got_1[1, 1] + got_1[1, 2]
    copies = []
    for k in range(3):
        copies.append(send(acc_1.at[0, lax.rem(y + k + 1, NY)], got_2.at[0, k], sems, 7 + k, ys[k]))
        copies.append(send(acc_1.at[1, lax.rem(x + k + 1, NX)], got_2.at[1, k], sems, 10 + k, xs[k]))
    for copy in copies:
        copy.wait()
    acc_2[pl.ds(0, TILES)] = acc_1[0, y] + got_2[0, 0] + got_2[0, 1] + got_2[0, 2]
    acc_2[pl.ds(TILES, TILES)] = acc_1[1, x] + got_2[1, 0] + got_2[1, 1] + got_2[1, 2]
    acc_2[pl.ds(2 * TILES, 24 - 2 * TILES)] = jnp.zeros((24 - 2 * TILES, 8, 128), jnp.float32)
    copies = []
    for k in range(7):
        copies.append(send(acc_2.at[pl.ds(3 * lax.rem(z + k + 1, NZ), 3)], got_z.at[k], sems, 13 + k, zs[k]))
    for copy in copies:
        copy.wait()
    own = acc_2[pl.ds(3 * z, 3)]
    for k in range(7):
        own = own + got_z[k]
    full_z[pl.ds(3 * z, 3)] = own
    mine = full_z.at[pl.ds(3 * z, 3)]
    copies = [send(mine, mine, sems, 20 + k, zs[k]) for k in range(7)]
    for copy in copies:
        copy.wait()
    out_ref[c, 0, x, y] = full_z[pl.ds(0, TILES)]
    out_ref[c, 1, y, x] = full_z[pl.ds(TILES, TILES)]
    first, second = out_ref.at[c, 0, x, y], out_ref.at[c, 1, y, x]
    copies = []
    for k in range(3):
        copies.append(send(first, first, sems, 27 + k, ys[k]))
        copies.append(send(second, second, sems, 30 + k, xs[k]))
    for copy in copies:
        copy.wait()
    first, second = out_ref.at[c, 0, x], out_ref.at[c, 1, y]
    copies = []
    for k in range(3):
        copies.append(send(first, first, sems, 33 + k, xs[k]))
        copies.append(send(second, second, sems, 36 + k, ys[k]))
    for copy in copies:
        copy.wait()
    send(out_ref.at[c], out_ref.at[c], sems, 39, across).wait()


def all_sum(packed, collective_id):
    vmem = pl.BlockSpec(memory_space=pltpu.VMEM)
    shape = (NC, 2, 4, 4, TILES, 8, 128)
    f32 = jnp.float32
    out = pl.pallas_call(
        all_sum_kernel,
        out_shape=jax.ShapeDtypeStruct(shape, f32),
        in_specs=[vmem],
        out_specs=vmem,
        scratch_shapes=[
            pltpu.VMEM(shape[1:], f32),
            pltpu.VMEM(shape[1:], f32),
            pltpu.VMEM((2, 3, 4, TILES, 8, 128), f32),
            pltpu.VMEM((2, 4, TILES, 8, 128), f32),
            pltpu.VMEM((2, 3, TILES, 8, 128), f32),
            pltpu.VMEM((24, 8, 128), f32),
            pltpu.VMEM((7, 3, 8, 128), f32),
            pltpu.VMEM((24, 8, 128), f32),
            pltpu.SemaphoreType.DMA((2, 40)),
        ],
        compiler_params=pltpu.CompilerParams(
            collective_id=collective_id, has_side_effects=True, vmem_limit_bytes=24 * MB
        ),
        name="all_sum",
    )(packed.reshape(shape))
    return out.reshape(36, BLK, BLK)


def scatter_sum_kernel(in_ref, out_ref, got_c, acc_a, acc_b, got_1, acc_1, got_2, acc_2, got_z, sems):
    x, y, z, c = place()
    here = (x, y, z, c)
    across = device(x, y, z, 1 - c)
    xs, ys, zs = x_peers(*here), y_peers(*here), z_peers(*here)
    meet([across] + xs + ys + zs)
    send(in_ref.at[:, :, :, 1 - c], got_c, sems, 0, across).wait()

    def add_core(step, carry):
        i = lax.div(step, NY)
        j = lax.rem(step, NY)
        both = in_ref[i, j, :, c] + got_c[i, j]
        acc_a[i, j] = both[:, :, :512]
        acc_b[j, i] = both[:, :, 512:]
        return carry

    lax.fori_loop(0, NX * NY, add_core, 0)
    copies = []
    for k in range(3):
        copies.append(send(acc_a.at[lax.rem(x + k + 1, NX)], got_1.at[0, k], sems, 1 + k, xs[k]))
        copies.append(send(acc_b.at[lax.rem(y + k + 1, NY)], got_1.at[1, k], sems, 4 + k, ys[k]))
    for copy in copies:
        copy.wait()

    def add_first(j, carry):
        acc_1[0, j] = acc_a[x, j] + got_1[0, 0, j] + got_1[0, 1, j] + got_1[0, 2, j]
        acc_1[1, j] = acc_b[y, j] + got_1[1, 0, j] + got_1[1, 1, j] + got_1[1, 2, j]
        return carry

    lax.fori_loop(0, 4, add_first, 0)
    copies = []
    for k in range(3):
        copies.append(send(acc_1.at[0, lax.rem(y + k + 1, NY)], got_2.at[0, k], sems, 7 + k, ys[k]))
        copies.append(send(acc_1.at[1, lax.rem(x + k + 1, NX)], got_2.at[1, k], sems, 10 + k, xs[k]))
    for copy in copies:
        copy.wait()
    acc_2[:, 0] = acc_1[0, y] + got_2[0, 0] + got_2[0, 1] + got_2[0, 2]
    acc_2[:, 1] = acc_1[1, x] + got_2[1, 0] + got_2[1, 1] + got_2[1, 2]
    copies = []
    for k in range(7):
        copies.append(send(acc_2.at[lax.rem(z + k + 1, NZ)], got_z.at[k], sems, 13 + k, zs[k]))
    for copy in copies:
        copy.wait()
    own = acc_2[z]
    for k in range(7):
        own = own + got_z[k]
    out_ref[:, :512] = own[0]
    out_ref[:, 512:] = own[1]


def scatter_sum(part, collective_id):
    vmem = pl.BlockSpec(memory_space=pltpu.VMEM)
    f32 = jnp.float32
    return pl.pallas_call(
        scatter_sum_kernel,
        out_shape=jax.ShapeDtypeStruct((8, 1024), f32),
        in_specs=[vmem],
        out_specs=vmem,
        scratch_shapes=[
            pltpu.VMEM((4, 4, 8, 8, 1024), f32),
            pltpu.VMEM((4, 4, 8, 8, 512), f32),
            pltpu.VMEM((4, 4, 8, 8, 512), f32),
            pltpu.VMEM((2, 3, 4, 8, 8, 512), f32),
            pltpu.VMEM((2, 4, 8, 8, 512), f32),
            pltpu.VMEM((2, 3, 8, 8, 512), f32),
            pltpu.VMEM((8, 2, 8, 512), f32),
            pltpu.VMEM((7, 2, 8, 512), f32),
            pltpu.SemaphoreType.DMA((2, 20)),
        ],
        compiler_params=pltpu.CompilerParams(
            collective_id=collective_id, has_side_effects=True, vmem_limit_bytes=40 * MB
        ),
        name="scatter_sum",
    )(part.reshape(NX, NY, NZ, NC, 8, 1024))


def pack(square):
    return jnp.stack(
        [square[i * BLK : (i + 1) * BLK, j * BLK : (j + 1) * BLK] for i in range(8) for j in range(i + 1)]
    )


def unpack(blocks):
    rows = []
    at = 0
    for i in range(8):
        row = [blocks[at + j] for j in range(i + 1)]
        at += i + 1
        if i < 7:
            row.append(jnp.zeros((BLK, (7 - i) * BLK), jnp.float32))
        rows.append(jnp.concatenate(row, axis=1))
    return jnp.concatenate(rows, axis=0)


def body(hidden, weight, partners):
    local_rows = hidden.shape[0]
    total_rows = local_rows * lax.axis_size("group") * lax.axis_size("dp")
    embedded = jnp.dot(hidden, weight, preferred_element_type=jnp.float32)
    sums = tile_sum(jnp.sum(embedded, axis=0).reshape(8, 128), 0)
    centered = embedded - sums.reshape(1, -1) / total_rows
    scatter = unpack(all_sum(pack(jnp.dot(centered.T, centered, precision=highest)), 1))
    cov = jnp.tril(scatter) / (total_rows - 1)
    factor = jnp.linalg.cholesky(cov, symmetrize_input=False)
    inv = lax.linalg.triangular_solve(
        factor, jnp.eye(1024, dtype=jnp.float32), left_side=True, lower=True
    )
    white = jnp.dot(centered, inv.T, precision=highest)
    whitened = white.astype(jnp.bfloat16)
    row_norm = jnp.sqrt(jnp.sum(white * white, axis=1, keepdims=True) + epsilon)
    unit = white / row_norm
    pick = (partners[0][:, None] == jnp.arange(local_rows, dtype=jnp.int32)[None, :]).astype(jnp.float32)
    grad_unit = 2.0 * (2.0 * unit - jnp.dot(pick + pick.T, unit, precision=highest))
    inner_prod = jnp.sum(white * grad_unit, axis=1, keepdims=True)
    grad_white = grad_unit / row_norm - white * (inner_prod / row_norm**3)
    grad_sums = tile_sum(jnp.sum(grad_white, axis=0).reshape(8, 128), 2).reshape(1, -1)
    pair = unpack(all_sum(pack(jnp.dot(grad_white.T, white, precision=highest)), 3))
    low = jnp.tril(pair, -1)
    mirror = low + low.T + pair * jnp.eye(1024, dtype=jnp.float32)
    total = grad_white - grad_sums / total_rows - jnp.dot(white, mirror, precision=highest) / (total_rows - 1)
    grad_z = jnp.dot(total, inv, precision=highest).astype(jnp.bfloat16)
    part = lax.dot_general(hidden, grad_z, (((0,), (0,)), ((), ())), preferred_element_type=jnp.float32)
    grad_weight = scatter_sum(part, 4)
    grad_hidden = jnp.dot(grad_z, weight.T, preferred_element_type=jnp.float32).astype(jnp.bfloat16)
    return (whitened, grad_weight, grad_hidden)


def solution(mesh):
    return jax.shard_map(
        body,
        mesh=mesh,
        in_specs=(P(("group", "dp"), None), P(), P(("group", "dp"), None)),
        out_specs=(P(("group", "dp"), None), P(("group", "dp"), None), P(("group", "dp"), None)),
        check_vma=False,
    )
```

time: 2480 us -> 763 us (0.31)
  waiting for transfers between devices: 1790 us -> 0 us
  Pallas kernels: 0 us -> 177 us
  blocking collectives: 155 us -> 0 us
  local copies, waits for them, and re-layouts: 96.8 us -> 211 us
  matrix products: 136 us -> 80.7 us
    unnamed x4 -> x0, waiting for transfers between devices: 1270 us -> none
    psum x2 -> x0, waiting for transfers between devices: 521 us -> none  [the longest x1 262 us: body(): lax.psum(jnp.dot(centered.T, centered, precision=highest), ('group', 'dp'))]
    pallas_call x0 -> x5, Pallas kernels: none -> 177 us  [the longest x2 91.1 us: all_sum(): pl.pallas_call(all_sum_kernel, out_shape=jax.ShapeDtypeStruct(shape, f32)...]
    psum x2 -> x0, blocking collectives: 155 us -> none  [the longest x1 79.1 us: body(): mean_row = lax.psum(jnp.sum(embedded, axis=0), ('group', 'dp')) / total_rows]
    unnamed x76 -> x245, local copies, waits for them, and re-layouts: 24.9 us -> 149 us
    another operation x74 -> x29, matrix products: 102 us -> 44.9 us  [the longest x14 23.1 us: body(): factor = jnp.linalg.cholesky(cov, symmetrize_input=False)]
    gather x5 -> x0, local copies, waits for them, and re-layouts: 25.5 us -> none  [the longest x1 17.3 us: body(): jnp.diag(pair_moment)]
  transfers between devices with their start and end apart: 3 -> 0, of which waited for: 3 -> 0; matrix products, arithmetic and copies ran while one was open for 1% -> 0% of each run, Pallas kernels for 0% -> 0%
where the time goes in v1:
time: 763 us; the launch traced here: 748 us
  other arithmetic  272 us (36%)
  local copies, waits for them, and re-layouts  211 us (28%)
  Pallas kernels  177 us (23%)
  matrix products  80.7 us (11%)
  between operations  7.7 us (1%)
    another operation x30, other arithmetic, body(): factor = jnp.linalg.cholesky(cov, symmetrize_input=False)  169 us
    unnamed x245, local copies, waits for them, and re-layouts  149 us
    pallas_call x2, Pallas kernels, all_sum(): pl.pallas_call(all_sum_kernel, out_shape=jax.ShapeDtypeStruct(shape, f32)...  91.1 us
    another operation x3, other arithmetic, body(): lax.linalg.triangular_solve(factor, jnp.eye(1024, dtype=jnp.float32), lef...  83.6 us
    pallas_call x1, Pallas kernels, scatter_sum(): pl.pallas_call(scatter_sum_kernel, out_shape=jax.ShapeDtypeStruct((8, 102...  52.1 us
    pallas_call x2, Pallas kernels, tile_sum(): pl.pallas_call(tile_sum_kernel, out_shape=jax.ShapeDtypeStruct((8, 128),...  33.8 us
    another operation x14, matrix products, body(): factor = jnp.linalg.cholesky(cov, symmetrize_input=False)  23.1 us
    another operation x26, local copies, waits for them, and re-layouts  22.8 us

profile of v1, /device:TPU:0, one launch (start us, length us, event | category | flops | bytes accessed | tf_op | source)
XLA Modules:
  0.0 748.4 jit_solution(14890013125587331597)
XLA Ops:
  1.9 4.0 fusion.104
  5.9 18.6 %tile_sum.2 = f32[8,128]{1,0:T(8,128)} custom-call(f32[8,128]{1,0:T(8,128)} %bitcast.571), custom_call_target="tpu_custom_call" | custom-call | tf_op jit(solution)/shard_map/tile_sum/pallas_call | solution.py:84
  25.2 3.7 fusion.41
  29.7 46.7 %all_sum.2 = f32[2,2,4,4,9,8,128]{6,5,4,3,2,1,0:T(8,128)S(1)} custom-call(f32[2,2,4,4,9,8,128]{6,5,4,3,2,1,0:T(8,128)S(1)} %bitcast.556), custom_call_target="tpu_custom_call" | custom-call | tf_op jit(solution)/shard_map/all_sum/pallas_call | solution.py:165
  83.8 1.9 maximum_dynamic-update-slice_fusion.1
  90.4 1.9 maximum_dynamic-update-slice_fusion
  153.1 5.8 copy.105
  158.8 2.7 select_multiply_fusion
  161.6 1.9 copy-done.6
  163.5 11.7 %cholesky.221 = f32[128,128]{1,0:T(8,128)S(1)} custom-call(f32[128,128]{1,0:T(8,128)S(1)} %cholesky.574), custom_call_target="Cholesky" | custom-call | tf_op jit(solution)/shard_map/jit(cholesky)/cholesky | solution.py:291
  175.2 2.5 cholesky.250
  178.0 9.8 %custom-call.62 = f32[1,128,128]{1,2,0:T(8,128)S(1)} custom-call(f32[1,128,128]{2,1,0:T(8,128)S(1)} %copy.108), custom_call_target="InvertDiagBlocksLowerTriangular" | custom-call | tf_op jit(solution)/shard_map/jit(cholesky)/cholesky | solution.py:291
  187.8 2.4 constant_dynamic-update-slice_fusion.116
  191.8 11.7 %cholesky.241 = f32[128,128]{1,0:T(8,128)S(1)} custom-call(f32[128,128]{1,0:T(8,128)S(1)} %cholesky.578), custom_call_target="Cholesky" | custom-call | tf_op jit(solution)/shard_map/jit(cholesky)/cholesky | solution.py:291
  206.4 9.9 %custom-call.63 = f32[1,128,128]{1,2,0:T(8,128)S(1)} custom-call(f32[1,128,128]{2,1,0:T(8,128)S(1)} %copy.111), custom_call_target="InvertDiagBlocksLowerTriangular" | custom-call | tf_op jit(solution)/shard_map/jit(cholesky)/cholesky | solution.py:291
  217.6 2.1 convolution_subtract_fusion.7
  219.7 11.7 %cholesky.463 = f32[128,128]{1,0:T(8,128)S(1)} custom-call(f32[128,128]{1,0:T(8,128)S(1)} %cholesky.583), custom_call_target="Cholesky" | custom-call | tf_op jit(solution)/shard_map/jit(cholesky)/cholesky | solution.py:291
  233.6 9.8 %custom-call.64 = f32[1,128,128]{1,2,0:T(8,128)S(1)} custom-call(f32[1,128,128]{2,1,0:T(8,128)S(1)} %copy.114), custom_call_target="InvertDiagBlocksLowerTriangular" | custom-call | tf_op jit(solution)/shard_map/jit(cholesky)/cholesky | solution.py:291
  244.6 2.3 convolution_subtract_fusion.8
  247.0 11.9 %cholesky.482 = f32[128,128]{1,0:T(8,128)S(1)} custom-call(f32[128,128]{1,0:T(8,128)S(1)} %cholesky.588), custom_call_target="Cholesky" | custom-call | tf_op jit(solution)/shard_map/jit(cholesky)/cholesky | solution.py:291
  261.2 9.8 %custom-call.65 = f32[1,128,128]{1,2,0:T(8,128)S(1)} custom-call(f32[1,128,128]{2,1,0:T(8,128)S(1)} %copy.117), custom_call_target="InvertDiagBlocksLowerTriangular" | custom-call | tf_op jit(solution)/shard_map/jit(cholesky)/cholesky | solution.py:291
  272.1 2.3 convolution_subtract_fusion.9
  274.4 11.7 %cholesky.501 = f32[128,128]{1,0:T(8,128)S(1)} custom-call(f32[128,128]{1,0:T(8,128)S(1)} %cholesky.593), custom_call_target="Cholesky" | custom-call | tf_op jit(solution)/shard_map/jit(cholesky)/cholesky | solution.py:291
  288.4 10.2 %custom-call.66 = f32[1,128,128]{1,2,0:T(8,128)S(1)} custom-call(f32[1,128,128]{2,1,0:T(8,128)S(1)} %copy.120), custom_call_target="InvertDiagBlocksLowerTriangular" | custom-call | tf_op jit(solution)/shard_map/jit(cholesky)/cholesky | solution.py:291
  299.6 2.3 convolution_subtract_fusion.10
  301.9 11.7 %cholesky.521 = f32[128,128]{1,0:T(8,128)S(1)} custom-call(f32[128,128]{1,0:T(8,128)S(1)} %cholesky.598), custom_call_target="Cholesky" | custom-call | tf_op jit(solution)/shard_map/jit(cholesky)/cholesky | solution.py:291
  315.9 9.8 %custom-call.67 = f32[1,128,128]{1,2,0:T(8,128)S(1)} custom-call(f32[1,128,128]{2,1,0:T(8,128)S(1)} %copy.123), custom_call_target="InvertDiagBlocksLowerTriangular" | custom-call | tf_op jit(solution)/shard_map/jit(cholesky)/cholesky | solution.py:291
  326.6 2.0 convolution_subtract_fusion.11
  328.7 11.9 %cholesky.541 = f32[128,128]{1,0:T(8,128)S(1)} custom-call(f32[128,128]{1,0:T(8,128)S(1)} %cholesky.603), custom_call_target="Cholesky" | custom-call | tf_op jit(solution)/shard_map/jit(cholesky)/cholesky | solution.py:291
  342.8 9.8 %custom-call.68 = f32[1,128,128]{1,2,0:T(8,128)S(1)} custom-call(f32[1,128,128]{2,1,0:T(8,128)S(1)} %copy.126), custom_call_target="InvertDiagBlocksLowerTriangular" | custom-call | tf_op jit(solution)/shard_map/jit(cholesky)/cholesky | solution.py:291
  353.4 1.8 convolution_subtract_fusion.12
  355.2 11.7 %cholesky.559 = f32[128,128]{1,0:T(8,128)S(1)} custom-call(f32[128,128]{1,0:T(8,128)S(1)} %convolution_subtract_fusion.12), custom_call_target="Cholesky" | custom-call | tf_op jit(solution)/shard_map/jit(cholesky)/cholesky | solution.py:291
  369.1 4.8 select_select_fusion
  373.9 23.0 %while.1 = (s32[]{:T(128)}, f32[1024,1024]{1,0:T(8,128)}, s32[8,2]{0,1:T(2,128)S(1)}, f32[8,128,128]{2,1,0:T(8,128)S(1)}, s32[]{:T(128)}) while((s32[]{:T(128)}, f32[1024,1024]{1,0:T(8,128)}, s32[8,2]{0,1:T(2,128)S(1)}, f32[8,128,128]{2,1,0:T(8,128)S(1)}, s32[]{:T(128)}) %tuple.126), condition=%wide.while_cond, body=%wide.while_body.sunk | while | flops 2 | bytes 131181 | solution.py:292
  374.5 2.3 bitcast_dynamic-update-slice_fusion.52
  377.4 2.3 bitcast_dynamic-update-slice_fusion.52
  380.2 2.3 bitcast_dynamic-update-slice_fusion.52
  383.1 2.3 bitcast_dynamic-update-slice_fusion.52
  386.0 2.3 bitcast_dynamic-update-slice_fusion.52
  388.9 2.3 bitcast_dynamic-update-slice_fusion.52
  391.8 2.3 bitcast_dynamic-update-slice_fusion.52
  394.7 2.2 bitcast_dynamic-update-slice_fusion.52
  396.9 78.8 %custom-call.69 = f32[8,128,128]{1,2,0:T(8,128)S(1)} custom-call(f32[8,128,128]{2,1,0:T(8,128)S(1)} %get-tuple-element.10), custom_call_target="InvertDiagBlocksLowerTriangular" | custom-call | tf_op jit(solution)/shard_map/triangular_solve | solution.py:292
  481.6 2.0 fusion.28
  484.4 2.2 fusion.31
  487.3 2.6 convolution_subtract_fusion.3
  490.7 2.8 convolution_subtract_fusion.2
  494.2 3.7 convolution_subtract_fusion.4
  498.5 3.8 multiply_reduce_fusion.1
  504.8 3.9 fusion.97
  509.4 44.3 %all_sum.3 = f32[2,2,4,4,9,8,128]{6,5,4,3,2,1,0:T(8,128)S(1)} custom-call(f32[2,2,4,4,9,8,128]{6,5,4,3,2,1,0:T(8,128)S(1)} %bitcast.557), custom_call_target="tpu_custom_call" | custom-call | tf_op jit(solution)/shard_map/all_sum/pallas_call | solution.py:165
  561.0 1.9 maximum_dynamic-update-slice_fusion.3
  567.6 1.9 maximum_dynamic-update-slice_fusion.2
  630.4 5.2 fusion.4
  635.5 5.4 copy.165
  640.9 5.5 copy.166
  648.1 15.1 %tile_sum.3 = f32[8,128]{1,0:T(8,128)} custom-call(f32[8,128]{1,0:T(8,128)} %bitcast.570), custom_call_target="tpu_custom_call" | custom-call | tf_op jit(solution)/shard_map/tile_sum/pallas_call | solution.py:84
  663.9 8.4 %fusion.25 = f32[256,1024]{1,0:T(8,128)S(1)} fusion(f32[256,1024]{1,0:T(8,128)S(1)} %copy-done.3, f32[1024,1024]{1,0:T(8,128)} %copy.165, f32[1024,1024]{0,1:T(8,128)} %fusion.4, f32[1024,1024]{1,0:T(8,128)} %copy.166, f32[1024]{0:T(1024)S(1)} %multiply_bitcast_fusion, f32[256]{0:T(256)S(1)} %fusion.92, f32[256,1024]{1,0:T(8,128)S(1)} %copy-done.8, ...), kind=kOutput, calls=%fused_computation.33 | convolution fusion | flops 3226992640 | bytes 15734784 | tf_op jit(solution)/shard_map/dot_general | solution.py:307
  672.3 3.7 convolution_convert_fusion.1
  676.0 4.5 convolution_bitcast_fusion
  680.6 9.3 %copy.167 = f32[2048,1024]{1,0:T(8,128)} copy(f32[2048,1024]{0,1:T(8,128)} %convolution_bitcast_fusion) | data formatting | bytes 16777216 | tf_op jit(solution)/shard_map/dot_general | solution.py:309
  689.8 3.4 copy-done.1
  693.2 52.1 %scatter_sum.1 = f32[8,1024]{1,0:T(8,128)S(1)} custom-call(f32[4,4,8,2,8,1024]{5,4,3,2,1,0:T(8,128)S(1)} %bitcast.551), custom_call_target="tpu_custom_call" | custom-call | tf_op jit(solution)/shard_map/scatter_sum/pallas_call | solution.py:242
  745.3 2.3 convolution_convert_fusion
  (344 shorter events, 186.5 us)
Async XLA Ops:
  0.6 1.2 copy-start
  5.9 23.5 %copy-start.9 = (f32[256,1024]{1,0:T(8,128)}, f32[256,1024]{1,0:T(8,128)S(1)}, u32[]{:S(2)}) copy-start(f32[256,1024]{1,0:T(8,128)S(1)} %get-tuple-element.135) | copy-start | bytes 3145732
  125.0 25.1 %copy-start.13 = (f32[1,128,128]{2,1,0:T(8,128)S(1)}, f32[1,128,128]{2,1,0:T(8,128)}, u32[]{:S(2)}) copy-start(f32[1,128,128]{2,1,0:T(8,128)} %get-tuple-element.60) | copy-start | bytes 196612
  125.0 25.8 %copy-start.11 = (f32[1,128,128]{2,1,0:T(8,128)S(1)}, f32[1,128,128]{2,1,0:T(8,128)}, u32[]{:S(2)}) copy-start(f32[1,128,128]{2,1,0:T(8,128)} %get-tuple-element.59) | copy-start | bytes 196612
  161.5 1.9 copy-start.6
  493.5 5.0 copy-start.10
  497.9 4.5 copy-start.16
  498.5 5.3 copy-start.4
  502.3 1.5 copy-start.2
  503.8 1.0 copy-start.7
  602.3 25.0 %copy-start.14 = (f32[1,128,128]{2,1,0:T(8,128)S(1)}, f32[1,128,128]{2,1,0:T(8,128)}, u32[]{:S(2)}) copy-start(f32[1,128,128]{2,1,0:T(8,128)} %get-tuple-element.24) | copy-start | bytes 196612
  602.3 25.8 %copy-start.12 = (f32[1,128,128]{2,1,0:T(8,128)S(1)}, f32[1,128,128]{2,1,0:T(8,128)}, u32[]{:S(2)}) copy-start(f32[1,128,128]{2,1,0:T(8,128)} %get-tuple-element.23) | copy-start | bytes 196612
  640.9 5.5 copy-start.3
  640.9 5.5 copy-start.8
  663.9 8.4 %copy-start.5 = (f32[1024,1024]{1,0:T(8,128)S(1)}, f32[1024,1024]{1,0:T(8,128)}, u32[]{:S(2)}) copy-start(f32[1024,1024]{1,0:T(8,128)} %copy-done.4) | copy-start | bytes 12582916
  689.8 3.4 copy-start.1
  693.2 52.1 %copy-start.15 = (bf16[2048,1024]{1,0:T(8,128)(2,1)S(1)}, bf16[2048,1024]{1,0:T(8,128)(2,1)}, u32[]{:S(2)}) copy-start(bf16[2048,1024]{1,0:T(8,128)(2,1)} %param.4) | copy-start | bytes 12582916

commit v2 on v1

--- a/solution.py
+++ b/solution.py
@@ -1,3 +1,5 @@
+import functools
+
 import jax
 import jax.numpy as jnp
 from jax import lax
@@ -262,22 +264,259 @@
     )(part.reshape(NX, NY, NZ, NC, 8, 1024))
 
 
-def pack(square):
-    return jnp.stack(
-        [square[i * BLK : (i + 1) * BLK, j * BLK : (j + 1) * BLK] for i in range(8) for j in range(i + 1)]
-    )
-
-
-def unpack(blocks):
-    rows = []
+def dots(a, b, ca=1, cb=0):
+    return lax.dot_general(a, b, (((ca,), (cb,)), ((), ())), precision=highest, preferred_element_type=jnp.float32)
+
+
+def inverse_factor_block(pan):
+    sub = lax.broadcasted_iota(jnp.int32, (8, BLK), 0)
+    lane = lax.broadcasted_iota(jnp.int32, (8, BLK), 1)
+
+    def over_sublanes(tile, k):
+        return jnp.broadcast_to(tile[k : k + 1, :], (8, BLK))
+
+    def over_lanes(tile, k):
+        return jnp.broadcast_to(tile[:, k : k + 1], (8, BLK))
+
+    pan = list(pan)
+    for p in range(16):
+        base = 8 * p
+        inside = (lane >= base) & (lane < base + 8)
+        own = pan[p]
+        cols = [over_lanes(own, base + k) for k in range(8)]
+        low = {(i, k): over_sublanes(cols[k], i) for k in range(8) for i in range(k, 8)}
+        own = jnp.where(inside, jnp.where(lane - base == sub, 1.0, 0.0), own)
+        rows = [over_sublanes(own, k) for k in range(8)]
+        ahead = p + 1 < 16
+        if ahead:
+            left = [over_lanes(pan[p + 1], base + k) for k in range(8)]
+            after = jnp.where(inside, 0.0, pan[p + 1])
+        scale = []
+        for k in range(8):
+            rs = lax.rsqrt(low[k, k])
+            scale.append(rs)
+            rows[k] = rows[k] * rs
+            for i in range(k + 1, 8):
+                low[i, k] = low[i, k] * rs
+            if ahead:
+                left[k] = left[k] * rs
+                after = after - left[k] * rows[k]
+            for i in range(k + 1, 8):
+                for m in range(k + 1, i + 1):
+                    low[i, m] = low[i, m] - low[i, k] * low[m, k]
+                rows[i] = rows[i] - low[i, k] * rows[k]
+                if ahead:
+                    left[i] = left[i] - left[k] * low[i, k]
+        done = rows[0]
+        for k in range(1, 8):
+            done = jnp.where(sub == k, rows[k], done)
+        pan[p] = done
+        if ahead:
+            pan[p + 1] = after
+        if p + 2 < 16:
+            back = [None] * 8
+            for k in range(7, -1, -1):
+                t = rows[k]
+                for m in range(k + 1, 8):
+                    t = t - low[m, k] * back[m]
+                back[k] = t * scale[k]
+            for q in range(p + 2, 16):
+                t = jnp.where(inside, 0.0, pan[q])
+                for k in range(8):
+                    t = t - over_lanes(pan[q], base + k) * back[k]
+                pan[q] = t
+    return [jnp.where(lane <= sub + 8 * p, pan[p], 0.0) for p in range(16)]
+
+
+def inverse_factor_kernel(inv_count, in_ref, out_ref, inv_ref, row_ref):
     at = 0
     for i in range(8):
-        row = [blocks[at + j] for j in range(i + 1)]
-        at += i + 1
-        if i < 7:
-            row.append(jnp.zeros((BLK, (7 - i) * BLK), jnp.float32))
-        rows.append(jnp.concatenate(row, axis=1))
-    return jnp.concatenate(rows, axis=0)
+        for j in range(i + 1):
+            block = in_ref[at] * inv_count
+            if i == j:
+                r = lax.broadcasted_iota(jnp.int32, (BLK, BLK), 0)
+                l = lax.broadcasted_iota(jnp.int32, (BLK, BLK), 1)
+                block = jnp.where(r >= l, block, block.T)
+                out_ref[i * BLK : (i + 1) * BLK, j * BLK : (j + 1) * BLK] = block
+            else:
+                out_ref[i * BLK : (i + 1) * BLK, j * BLK : (j + 1) * BLK] = block
+                out_ref[j * BLK : (j + 1) * BLK, i * BLK : (i + 1) * BLK] = block.T
+            at += 1
+
+    lane = lax.broadcasted_iota(jnp.int32, (BLK, 1024), 1)
+
+    def step(i, carry):
+        own = pl.ds(pl.multiple_of(i * BLK, BLK), BLK)
+        pans = [out_ref[pl.ds(pl.multiple_of(i * BLK + 8 * p, 8), 8), own] for p in range(16)]
+        for p, tile in enumerate(inverse_factor_block(pans)):
+            inv_ref[8 * p : 8 * p + 8, :] = tile
+        inv = inv_ref[...]
+        row_ref[...] = dots(inv, out_ref[own, :])
+        row_ref[:, own] = inv
+        out_ref[own, :] = jnp.where(lane < (i + 1) * BLK, row_ref[...], 0.0)
+
+        def lower(j, inner):
+            its = pl.ds(pl.multiple_of(j * BLK, BLK), BLK)
+            left = dots(out_ref[its, own], inv_ref[...], 1, 1)
+            out_ref[its, own] = jnp.zeros((BLK, BLK), jnp.float32)
+            out_ref[its, :] = out_ref[its, :] - dots(left, row_ref[...])
+            return inner
+
+        lax.fori_loop(i + 1, 8, lower, 0)
+        return carry
+
+    lax.fori_loop(0, 8, step, 0)
+
+
+def inverse_factor(packed, count):
+    vmem = pl.BlockSpec(memory_space=pltpu.VMEM)
+    return pl.pallas_call(
+        functools.partial(inverse_factor_kernel, 1.0 / count),
+        out_shape=jax.ShapeDtypeStruct((1024, 1024), jnp.float32),
+        in_specs=[vmem], out_specs=vmem,
+        scratch_shapes=[pltpu.VMEM((BLK, BLK), jnp.float32), pltpu.VMEM((BLK, 1024), jnp.float32)],
+        compiler_params=pltpu.CompilerParams(vmem_limit_bytes=32 * MB),
+        name="inverse_factor",
+    )(packed)
+
+
+def store_lower(out_ref, a, b):
+    for half in range(4):
+        strip = dots(a[:, half * 256 : half * 256 + 256], b[:, : half * 256 + 256], 0, 0)
+        for i in (2 * half, 2 * half + 1):
+            for j in range(i + 1):
+                r = (i - 2 * half) * BLK
+                out_ref[i * (i + 1) // 2 + j] = strip[r : r + BLK, j * BLK : (j + 1) * BLK]
+
+
+def center_kernel(count, emb_ref, sum_ref, cent_ref, packed_ref):
+    cent = emb_ref[...] - sum_ref[...] * (1.0 / count)
+    cent_ref[...] = cent
+    store_lower(packed_ref, cent_ref, cent_ref)
+
+
+def center(embedded, sums, count):
+    vmem = pl.BlockSpec(memory_space=pltpu.VMEM)
+    f32 = jnp.float32
+    return pl.pallas_call(
+        functools.partial(center_kernel, count),
+        out_shape=(jax.ShapeDtypeStruct((256, 1024), f32), jax.ShapeDtypeStruct((36, BLK, BLK), f32)),
+        in_specs=[vmem] * 2,
+        out_specs=(vmem, vmem),
+        compiler_params=pltpu.CompilerParams(vmem_limit_bytes=32 * MB),
+        name="center",
+    )(embedded, sums)
+
+
+def white_kernel(cent_ref, inv_ref, partner_ref, whitened_ref, white_ref, grad_ref, packed_ref):
+    bf16 = jnp.bfloat16
+    for part in range(4):
+        stop = part * 256 + 256
+        white_ref[:, stop - 256 : stop] = dots(cent_ref[:, :stop], inv_ref[stop - 256 : stop, :stop], 1, 1)
+    white = white_ref[...]
+    whitened_ref[...] = white.astype(bf16)
+    row_norm = jnp.sqrt(jnp.sum(white * white, axis=1, keepdims=True) + epsilon)
+    unit = white / row_norm
+    ids = lax.broadcasted_iota(jnp.int32, (256, 256), 0)
+    pick = (ids == partner_ref[...]).astype(jnp.float32)
+    pick = (pick + pick.T).astype(bf16)
+    near = jnp.zeros_like(unit)
+    rest = unit
+    for _ in range(3):
+        term = rest.astype(bf16)
+        near = near + jnp.dot(pick, term, preferred_element_type=jnp.float32)
+        rest = rest - term.astype(jnp.float32)
+    grad_unit = 2.0 * (2.0 * unit - near)
+    inner_prod = jnp.sum(white * grad_unit, axis=1, keepdims=True)
+    grad = grad_unit / row_norm - white * (inner_prod / (row_norm * row_norm * row_norm))
+    grad_ref[...] = grad
+    store_lower(packed_ref, grad_ref, white_ref)
+    sums = jnp.sum(grad, axis=0, keepdims=True)
+    sub = lax.broadcasted_iota(jnp.int32, (8, BLK), 0)
+    lane = lax.broadcasted_iota(jnp.int32, (8, BLK), 1)
+    for i in range(8):
+        at = i * (i + 1) // 2 + i
+        own = jnp.broadcast_to(sums[:, i * BLK : (i + 1) * BLK], (8, BLK))
+        swapped = pltpu.roll(own, 64, 1)
+        tile = packed_ref[at, 0:8, :]
+        tile = jnp.where((lane >= 64) & (sub == 0), swapped, jnp.where((lane >= 64) & (sub == 1), own, tile))
+        packed_ref[at, 0:8, :] = tile
+
+
+def whiten(centered, inv, partners):
+    vmem = pl.BlockSpec(memory_space=pltpu.VMEM)
+    f32 = jnp.float32
+    return pl.pallas_call(
+        white_kernel,
+        out_shape=(
+            jax.ShapeDtypeStruct((256, 1024), jnp.bfloat16),
+            jax.ShapeDtypeStruct((256, 1024), f32),
+            jax.ShapeDtypeStruct((256, 1024), f32),
+            jax.ShapeDtypeStruct((36, BLK, BLK), f32),
+        ),
+        in_specs=[vmem] * 3,
+        out_specs=(vmem,) * 4,
+        compiler_params=pltpu.CompilerParams(vmem_limit_bytes=40 * MB),
+        name="whiten",
+    )(centered, inv, partners)
+
+
+def grads_kernel(count, white_ref, grad_ref, packed_ref, inv_ref, hidden_ref, weight_ref, gh_ref, part_ref, mirror, total, grad_z):
+    lane = lax.broadcasted_iota(jnp.int32, (1, BLK), 1)
+    r = lax.broadcasted_iota(jnp.int32, (BLK, BLK), 0)
+    l = lax.broadcasted_iota(jnp.int32, (BLK, BLK), 1)
+    scale = 1.0 / (count - 1)
+    for i in range(8):
+        for j in range(i + 1):
+            at = i * (i + 1) // 2 + j
+            block = packed_ref[at]
+            turned = block.T
+            rows, cols = slice(i * BLK, (i + 1) * BLK), slice(j * BLK, (j + 1) * BLK)
+            if i == j:
+                mirror[rows, cols] = jnp.where(r >= l, block, turned) * scale
+                first, second = packed_ref[at, 0:1, :], packed_ref[at, 1:2, :]
+                sums = jnp.where(lane < 64, pltpu.roll(first, 64, 1), second)
+                total[:, cols] = grad_ref[:, cols] - sums * (1.0 / count)
+            else:
+                mirror[rows, cols] = block * scale
+                mirror[cols, rows] = turned * scale
+    for part in range(4):
+        cols = slice(part * 256, part * 256 + 256)
+        total[:, cols] = total[:, cols] - dots(white_ref[...], mirror[:, cols])
+    for part in range(4):
+        start = part * 256
+        cols = slice(start, start + 256)
+        grad_z[:, cols] = dots(total[:, start:], inv_ref[start:, cols]).astype(jnp.bfloat16)
+
+    def chunk(k, carry):
+        own = pl.ds(pl.multiple_of(k * 256, 256), 256)
+        part_ref[own, :] = lax.dot_general(
+            hidden_ref[:, own], grad_z[...], (((0,), (0,)), ((), ())), preferred_element_type=jnp.float32
+        )
+        gh_ref[:, own] = lax.dot_general(
+            grad_z[...], weight_ref[own, :], (((1,), (1,)), ((), ())), preferred_element_type=jnp.float32
+        ).astype(jnp.bfloat16)
+        return carry
+
+    lax.fori_loop(0, 8, chunk, 0)
+
+
+def grads(white, grad, packed, inv, hidden, weight, count):
+    vmem = pl.BlockSpec(memory_space=pltpu.VMEM)
+    f32 = jnp.float32
+    return pl.pallas_call(
+        functools.partial(grads_kernel, count),
+        out_shape=(jax.ShapeDtypeStruct((256, 2048), jnp.bfloat16), jax.ShapeDtypeStruct((2048, 1024), f32)),
+        in_specs=[vmem] * 6,
+        out_specs=(vmem,) * 2,
+        scratch_shapes=[
+            pltpu.VMEM((1024, 1024), f32),
+            pltpu.VMEM((256, 1024), f32),
+            pltpu.VMEM((256, 1024), jnp.bfloat16),
+        ],
+        compiler_params=pltpu.CompilerParams(vmem_limit_bytes=48 * MB),
+        name="grads",
+    )(white, grad, packed, inv, hidden, weight)
 
 
 def body(hidden, weight, partners):
@@ -285,30 +524,11 @@
     total_rows = local_rows * lax.axis_size("group") * lax.axis_size("dp")
     embedded = jnp.dot(hidden, weight, preferred_element_type=jnp.float32)
     sums = tile_sum(jnp.sum(embedded, axis=0).reshape(8, 128), 0)
-    centered = embedded - sums.reshape(1, -1) / total_rows
-    scatter = unpack(all_sum(pack(jnp.dot(centered.T, centered, precision=highest)), 1))
-    cov = jnp.tril(scatter) / (total_rows - 1)
-    factor = jnp.linalg.cholesky(cov, symmetrize_input=False)
-    inv = lax.linalg.triangular_solve(
-        factor, jnp.eye(1024, dtype=jnp.float32), left_side=True, lower=True
-    )
-    white = jnp.dot(centered, inv.T, precision=highest)
-    whitened = white.astype(jnp.bfloat16)
-    row_norm = jnp.sqrt(jnp.sum(white * white, axis=1, keepdims=True) + epsilon)
-    unit = white / row_norm
-    pick = (partners[0][:, None] == jnp.arange(local_rows, dtype=jnp.int32)[None, :]).astype(jnp.float32)
-    grad_unit = 2.0 * (2.0 * unit - jnp.dot(pick + pick.T, unit, precision=highest))
-    inner_prod = jnp.sum(white * grad_unit, axis=1, keepdims=True)
-    grad_white = grad_unit / row_norm - white * (inner_prod / row_norm**3)
-    grad_sums = tile_sum(jnp.sum(grad_white, axis=0).reshape(8, 128), 2).reshape(1, -1)
-    pair = unpack(all_sum(pack(jnp.dot(grad_white.T, white, precision=highest)), 3))
-    low = jnp.tril(pair, -1)
-    mirror = low + low.T + pair * jnp.eye(1024, dtype=jnp.float32)
-    total = grad_white - grad_sums / total_rows - jnp.dot(white, mirror, precision=highest) / (total_rows - 1)
-    grad_z = jnp.dot(total, inv, precision=highest).astype(jnp.bfloat16)
-    part = lax.dot_general(hidden, grad_z, (((0,), (0,)), ((), ())), preferred_element_type=jnp.float32)
-    grad_weight = scatter_sum(part, 4)
-    grad_hidden = jnp.dot(grad_z, weight.T, preferred_element_type=jnp.float32).astype(jnp.bfloat16)
+    centered, packed = center(embedded, sums.reshape(1, -1), total_rows)
+    inv = inverse_factor(all_sum(packed, 1), total_rows - 1)
+    whitened, white, grad_white, packed = whiten(centered, inv, partners)
+    grad_hidden, part = grads(white, grad_white, all_sum(packed, 2), inv, hidden, weight, total_rows)
+    grad_weight = scatter_sum(part, 3)
     return (whitened, grad_weight, grad_hidden)
 
 

time: 763 us -> 263 us (0.34); the launches traced: 748 us -> 262 us
  other arithmetic: 272 us -> 0 us
  local copies, waits for them, and re-layouts: 211 us -> 4.69 us
  matrix products: 80.7 us -> 4.36 us
  Pallas kernels: 177 us -> 252 us
    another operation x33 -> x0, other arithmetic: 252 us -> none  [the longest x30 169 us: body(): factor = jnp.linalg.cholesky(cov, symmetrize_input=False)]
    unnamed x245 -> x11, local copies, waits for them, and re-layouts: 149 us -> 4.69 us
    pallas_call x0 -> x4, Pallas kernels: none -> 90 us  [the longest x1 63.7 us: inverse_factor(): pl.pallas_call(functools.partial(inverse_factor_kernel, 1.0 / count), out...]
    another operation x29 -> x0, matrix products: 44.9 us -> none  [the longest x14 23.1 us: body(): factor = jnp.linalg.cholesky(cov, symmetrize_input=False)]
    dot_general x8 -> x0, matrix products: 31.7 us -> none  [the longest x1 8.41 us: body(): jnp.dot(white, mirror, precision=highest) / (total_rows - 1)]
    another operation x59 -> x0, local copies, waits for them, and re-layouts: 31.2 us -> none
    pallas_call x2 -> x1, Pallas kernels: 33.8 us -> 18.6 us  [tile_sum(): pl.pallas_call(tile_sum_kernel, out_shape=jax.ShapeDtypeStruct((8, 128),...]
    concatenate x6 -> x0, local copies, waits for them, and re-layouts: 12.6 us -> none  [the longest x4 12.6 us: unpack(): return jnp.concatenate(rows, axis=0)]
where the time goes in v2:
time: 263 us; the launch traced here: 262 us
  Pallas kernels  252 us (96%)
  local copies, waits for them, and re-layouts  4.69 us (2%)
  matrix products  4.36 us (2%)
    pallas_call x2, Pallas kernels, all_sum(): pl.pallas_call(all_sum_kernel, out_shape=jax.ShapeDtypeStruct(shape, f32)...  90.9 us
    pallas_call x1, Pallas kernels, inverse_factor(): pl.pallas_call(functools.partial(inverse_factor_kernel, 1.0 / count), out...  63.7 us
    pallas_call x1, Pallas kernels, scatter_sum(): pl.pallas_call(scatter_sum_kernel, out_shape=jax.ShapeDtypeStruct((8, 102...  52.3 us
    pallas_call x1, Pallas kernels, tile_sum(): pl.pallas_call(tile_sum_kernel, out_shape=jax.ShapeDtypeStruct((8, 128),...  18.6 us
    pallas_call x1, Pallas kernels, grads(): pl.pallas_call(functools.partial(grads_kernel, count), out_shape=(jax.Sha...  17.3 us
    pallas_call x1, Pallas kernels, whiten(): pl.pallas_call(white_kernel, out_shape=(jax.ShapeDtypeStruct((256, 1024),...  6.63 us

profile of v2, /device:TPU:0, one launch (start us, length us, event | category | flops | bytes accessed | tf_op | source)
XLA Modules:
  0.0 261.7 jit_solution(17397969331807928809)
XLA Ops:
  0.6 4.4 %fusion = (f32[1024]{0:T(1024)}, f32[256,1024]{1,0:T(8,128)S(1)}) fusion(bf16[256,2048]{1,0:T(8,128)(2,1)} %hidden_ref.1, bf16[2048,1024]{1,0:T(8,128)(2,1)} %weight_ref.1), kind=kOutput, calls=%fused_computation | convolution fusion | flops 1074002944 | bytes 6295552 | tf_op jit(solution)/shard_map/dot_general | solution.py:525
  5.0 18.6 %tile_sum.1 = f32[8,128]{1,0:T(8,128)} custom-call(f32[8,128]{1,0:T(8,128)} %bitcast.15), custom_call_target="tpu_custom_call" | custom-call | tf_op jit(solution)/shard_map/tile_sum/pallas_call | solution.py:86
  23.6 0.0 copy-start.3
  23.7 0.7 copy-done.3
  24.3 2.5 center.1
  26.8 46.7 %all_sum.2 = f32[2,2,4,4,9,8,128]{6,5,4,3,2,1,0:T(8,128)S(1)} custom-call(f32[2,2,4,4,9,8,128]{6,5,4,3,2,1,0:T(8,128)S(1)} %bitcast.13), custom_call_target="tpu_custom_call" | custom-call | tf_op jit(solution)/shard_map/all_sum/pallas_call | solution.py:167
  73.5 0.0 copy-start.4
  73.6 63.7 %inverse_factor.1.inv_ref = f32[1024,1024]{1,0:T(8,128)S(1)} custom-call(f32[36,128,128]{2,1,0:T(8,128)S(1)} %bitcast.9), custom_call_target="tpu_custom_call" | custom-call | tf_op jit(solution)/shard_map/inverse_factor/pallas_call | solution.py:373
  137.2 0.0 copy-done.4
  137.2 0.0 copy-start
  137.2 0.0 copy-start.2
  137.3 6.6 %whiten.1 = (bf16[256,1024]{1,0:T(8,128)(2,1)}, f32[256,1024]{1,0:T(8,128)S(1)}, f32[256,1024]{1,0:T(8,128)S(1)}, f32[36,128,128]{2,1,0:T(8,128)S(1)}) custom-call(f32[256,1024]{1,0:T(8,128)S(1)} %get-tuple-element.11.cent_ref, f32[1024,1024]{1,0:T(8,128)S(1)} %inverse_factor.1.inv_ref, s32[1,256]{1,0:T(1,128)S(1)} %copy-done.4), custom_call_target="tpu_custom_call" | custom-call | tf_op jit(solution)/shard_map/whiten/pallas_call | solution.py:449
  143.9 44.1 %all_sum.3 = f32[2,2,4,4,9,8,128]{6,5,4,3,2,1,0:T(8,128)S(1)} custom-call(f32[2,2,4,4,9,8,128]{6,5,4,3,2,1,0:T(8,128)S(1)} %bitcast.12), custom_call_target="tpu_custom_call" | custom-call | tf_op jit(solution)/shard_map/all_sum/pallas_call | solution.py:167
  188.0 0.0 copy-done
  188.1 0.0 copy-done.2
  188.1 17.3 %grads.1 = (bf16[256,2048]{1,0:T(8,128)(2,1)}, f32[2048,1024]{1,0:T(8,128)}) custom-call(f32[256,1024]{1,0:T(8,128)S(1)} %get-tuple-element.14.white_ref, f32[256,1024]{1,0:T(8,128)S(1)} %get-tuple-element.15.grad_ref, f32[36,128,128]{2,1,0:T(8,128)S(1)} %bitcast.10, f32[1024,1024]{1,0:T(8,128)} %copy-done, bf16[256,2048]{1,0:T(8,128)(2,1)S(1)} %copy-done.2, ...), custom_call_target="tpu_custom_call" | custom-call | tf_op jit(solution)/shard_map/grads/pallas_call | solution.py:507
  205.4 0.0 copy-start.1
  205.4 3.4 %copy-done.1 = f32[2048,1024]{1,0:T(8,128)S(1)} copy-done((f32[2048,1024]{1,0:T(8,128)S(1)}, f32[2048,1024]{1,0:T(8,128)}, u32[]{:S(2)}) %copy-start.1) | copy-done | bytes 8388632
  208.7 52.3 %scatter_sum.1 = f32[8,1024]{1,0:T(8,128)S(1)} custom-call(f32[4,4,8,2,8,1024]{5,4,3,2,1,0:T(8,128)S(1)} %bitcast.11), custom_call_target="tpu_custom_call" | custom-call | tf_op jit(solution)/shard_map/scatter_sum/pallas_call | solution.py:244
  261.1 0.6 copy.7
Async XLA Ops:
  23.6 0.7 copy-start.3
  73.5 63.7 %copy-start.4 = (s32[1,256]{1,0:T(1,128)S(1)}, s32[1,256]{1,0:T(1,128)}, u32[]{:S(2)}) copy-start(s32[1,256]{1,0:T(1,128)} %partner_ref.1) | copy-start | bytes 3076
  137.2 50.8 %copy-start = (f32[1024,1024]{1,0:T(8,128)}, f32[1024,1024]{1,0:T(8,128)S(1)}, u32[]{:S(2)}) copy-start(f32[1024,1024]{1,0:T(8,128)S(1)} %inverse_factor.1.inv_ref) | copy-start | bytes 12582916
  137.2 50.8 %copy-start.2 = (bf16[256,2048]{1,0:T(8,128)(2,1)S(1)}, bf16[256,2048]{1,0:T(8,128)(2,1)}, u32[]{:S(2)}) copy-start(bf16[256,2048]{1,0:T(8,128)(2,1)} %hidden_ref.1) | copy-start | bytes 3145732
  205.4 3.4 %copy-start.1 = (f32[2048,1024]{1,0:T(8,128)S(1)}, f32[2048,1024]{1,0:T(8,128)}, u32[]{:S(2)}) copy-start(f32[2048,1024]{1,0:T(8,128)} %get-tuple-element.17) | copy-start | bytes 25165828

commit v3 on v0

v3 whole, which is shorter than its diff:
```python
import functools

import jax
import jax.numpy as jnp
from jax import lax
from jax.experimental import pallas as pl
from jax.experimental.pallas import tpu as pltpu
from jax.sharding import PartitionSpec as P

epsilon = 1e-06
highest = lax.Precision.HIGHEST
MESH = pl.DeviceIdType.MESH
NX, NY, NZ, NC = 4, 4, 8, 2
BLK = 128
MB = 1 << 20
f32, bf16 = jnp.float32, jnp.bfloat16


def place():
    dp = lax.axis_index("dp")
    x = lax.axis_index("group")
    return x, lax.div(dp, NZ * NC), lax.rem(lax.div(dp, NC), NZ), lax.rem(dp, NC)


def device(x, y, z, c):
    return (x, (y * NZ + z) * NC + c)


def send(src, dst, sems, slot, peer):
    copy = pltpu.make_async_remote_copy(
        src_ref=src,
        dst_ref=dst,
        send_sem=sems.at[0, slot],
        recv_sem=sems.at[1, slot],
        device_id=peer,
        device_id_type=MESH,
    )
    copy.start()
    return copy


def wait(copies):
    for copy in copies:
        copy.wait()


def dots(a, b, ca=1, cb=0):
    return lax.dot_general(a, b, (((ca,), (cb,)), ((), ())), precision=highest, preferred_element_type=f32)


def dot16(a, b, ca=1, cb=0):
    return lax.dot_general(a, b, (((ca,), (cb,)), ((), ())), preferred_element_type=f32)


def span(start, size):
    return pl.ds(pl.multiple_of(start, size), size)


def inverse_factor_block(pan):
    sub = lax.broadcasted_iota(jnp.int32, (8, BLK), 0)
    lane = lax.broadcasted_iota(jnp.int32, (8, BLK), 1)

    def over_sublanes(tile, k):
        return jnp.broadcast_to(tile[k : k + 1, :], (8, BLK))

    def over_lanes(tile, k):
        return jnp.broadcast_to(tile[:, k : k + 1], (8, BLK))

    pan = list(pan)
    for p in range(16):
        base = 8 * p
        inside = (lane >= base) & (lane < base + 8)
        own = pan[p]
        cols = [over_lanes(own, base + k) for k in range(8)]
        low = {(i, k): over_sublanes(cols[k], i) for k in range(8) for i in range(k, 8)}
        own = jnp.where(inside, jnp.where(lane - base == sub, 1.0, 0.0), own)
        rows = [over_sublanes(own, k) for k in range(8)]
        ahead = p + 1 < 16
        if ahead:
            left = [over_lanes(pan[p + 1], base + k) for k in range(8)]
            after = jnp.where(inside, 0.0, pan[p + 1])
        scale = []
        for k in range(8):
            rs = lax.rsqrt(low[k, k])
            scale.append(rs)
            rows[k] = rows[k] * rs
            for i in range(k + 1, 8):
                low[i, k] = low[i, k] * rs
            if ahead:
                left[k] = left[k] * rs
                after = after - left[k] * rows[k]
            for i in range(k + 1, 8):
                for m in range(k + 1, i + 1):
                    low[i, m] = low[i, m] - low[i, k] * low[m, k]
                rows[i] = rows[i] - low[i, k] * rows[k]
                if ahead:
                    left[i] = left[i] - left[k] * low[i, k]
        done = rows[0]
        for k in range(1, 8):
            done = jnp.where(sub == k, rows[k], done)
        pan[p] = done
        if ahead:
            pan[p + 1] = after
        if p + 2 < 16:
            back = [None] * 8
            for k in range(7, -1, -1):
                t = rows[k]
                for m in range(k + 1, 8):
                    t = t - low[m, k] * back[m]
                back[k] = t * scale[k]
            for q in range(p + 2, 16):
                t = jnp.where(inside, 0.0, pan[q])
                for k in range(8):
                    t = t - over_lanes(pan[q], base + k) * back[k]
                pan[q] = t
    return [jnp.where(lane <= sub + 8 * p, pan[p], 0.0) for p in range(16)]


def inverse_factor(scale, in_ref, out_ref, inv_ref, row_ref):
    for i in range(8):
        for j in range(i + 1):
            block = get_block(in_ref, i, j) * scale
            rows, cols = slice(i * BLK, (i + 1) * BLK), slice(j * BLK, (j + 1) * BLK)
            turned = block.T
            if i == j:
                r = lax.broadcasted_iota(jnp.int32, (BLK, BLK), 0)
                l = lax.broadcasted_iota(jnp.int32, (BLK, BLK), 1)
                out_ref[rows, cols] = jnp.where(r >= l, block, turned)
            else:
                out_ref[rows, cols] = block
                out_ref[cols, rows] = turned
    lane = lax.broadcasted_iota(jnp.int32, (BLK, 1024), 1)

    def step(i, carry):
        own = span(i * BLK, BLK)
        pans = [out_ref[span(i * BLK + 8 * p, 8), own] for p in range(16)]
        for p, tile in enumerate(inverse_factor_block(pans)):
            inv_ref[8 * p : 8 * p + 8, :] = tile
        inv = inv_ref[...]
        row_ref[...] = dots(inv, out_ref[own, :])
        row_ref[:, own] = inv
        out_ref[own, :] = jnp.where(lane < (i + 1) * BLK, row_ref[...], 0.0)

        def lower(j, inner):
            its = span(j * BLK, BLK)
            left = dots(out_ref[its, own], inv_ref[...], 1, 1)
            out_ref[its, own] = jnp.zeros((BLK, BLK), f32)
            out_ref[its, :] = out_ref[its, :] - dots(left, row_ref[...])
            return inner

        lax.fori_loop(i + 1, 8, lower, 0)
        return carry

    lax.fori_loop(0, 8, step, 0)


def get_block(ref, i, j):
    at = i * (i + 1) // 2 + j
    return ref[16 * at : 16 * at + 16].reshape(BLK, BLK)


def store_lower(out_ref, a, b):
    for half in range(4):
        strip = dots(a[:, half * 256 : half * 256 + 256], b[:, : half * 256 + 256], 0, 0)
        for i in (2 * half, 2 * half + 1):
            for j in range(i + 1):
                r = (i - 2 * half) * BLK
                at = i * (i + 1) // 2 + j
                out_ref[16 * at : 16 * at + 16] = strip[r : r + BLK, j * BLK : (j + 1) * BLK].reshape(16, 8, BLK)


def tile_sum(here, tile, got, sems):
    x, y, z, c = here
    copies = []
    for k in range(1, NZ * NC):
        own = lax.rem(z * NC + c + k, NZ * NC)
        peer = device(x, y, lax.div(own, NC), lax.rem(own, NC))
        copies.append(send(tile.at[0], got.at[0, k - 1], sems, k - 1, peer))
    wait(copies)
    total = tile[0]
    for k in range(15):
        total = total + got[0, k]
    tile[1] = total
    copies = []
    for k in range(1, NX * NY):
        own = lax.rem(x * NY + y + k, NX * NY)
        peer = device(lax.div(own, NY), lax.rem(own, NY), z, c)
        copies.append(send(tile.at[1], got.at[1, k - 1], sems, 14 + k, peer))
    wait(copies)
    for k in range(15):
        total = total + got[1, k]
    return total


T = 9


def all_sum(here, in_ref, out_ref, acc, got_c, got_1, acc_1, got_2, acc_2, got_z, full_z, sems):
    x, y, z, c = here
    across = device(x, y, z, 1 - c)
    xs = [device(lax.rem(x + k, NX), y, z, c) for k in range(1, NX)]
    ys = [device(x, lax.rem(y + k, NY), z, c) for k in range(1, NY)]
    zs = [device(x, y, lax.rem(z + k, NZ), c) for k in range(1, NZ)]
    x_at = [lax.rem(x + k, NX) for k in range(1, NX)]
    y_at = [lax.rem(y + k, NY) for k in range(1, NY)]
    z_at = [lax.rem(z + k, NZ) for k in range(1, NZ)]
    send(in_ref.at[pl.ds((1 - c) * 288, 288)], got_c, sems, 0, across).wait()
    acc[...] = in_ref[pl.ds(c * 288, 288)] + got_c[...]
    copies = []
    for k in range(3):
        copies.append(send(acc.at[pl.ds(x_at[k] * 36, 36)], got_1.at[0, k], sems, 1 + k, xs[k]))
        copies.append(send(acc.at[pl.ds(144 + y_at[k] * 36, 36)], got_1.at[1, k], sems, 4 + k, ys[k]))
    wait(copies)
    acc_1[0] = acc[pl.ds(x * 36, 36)] + got_1[0, 0] + got_1[0, 1] + got_1[0, 2]
    acc_1[1] = acc[pl.ds(144 + y * 36, 36)] + got_1[1, 0] + got_1[1, 1] + got_1[1, 2]
    copies = []
    for k in range(3):
        copies.append(send(acc_1.at[0, pl.ds(y_at[k] * T, T)], got_2.at[0, k], sems, 7 + k, ys[k]))
        copies.append(send(acc_1.at[1, pl.ds(x_at[k] * T, T)], got_2.at[1, k], sems, 10 + k, xs[k]))
    wait(copies)
    acc_2[0:T] = acc_1[0, pl.ds(y * T, T)] + got_2[0, 0] + got_2[0, 1] + got_2[0, 2]
    acc_2[T : 2 * T] = acc_1[1, pl.ds(x * T, T)] + got_2[1, 0] + got_2[1, 1] + got_2[1, 2]
    acc_2[2 * T : 24] = jnp.zeros((24 - 2 * T, 8, 128), f32)
    wait([send(acc_2.at[pl.ds(3 * z_at[k], 3)], got_z.at[k], sems, 13 + k, zs[k]) for k in range(7)])
    own = acc_2[pl.ds(3 * z, 3)]
    for k in range(7):
        own = own + got_z[k]
    mine = full_z.at[pl.ds(3 * z, 3)]
    mine[...] = own
    wait([send(mine, mine, sems, 20 + k, zs[k]) for k in range(7)])
    base = c * 288
    first, second = out_ref.at[pl.ds(base + (x * 4 + y) * T, T)], out_ref.at[pl.ds(base + 144 + (y * 4 + x) * T, T)]
    first[...] = full_z[0:T]
    second[...] = full_z[T : 2 * T]
    copies = []
    for k in range(3):
        copies.append(send(first, first, sems, 27 + k, ys[k]))
        copies.append(send(second, second, sems, 30 + k, xs[k]))
    wait(copies)
    first, second = out_ref.at[pl.ds(base + x * 36, 36)], out_ref.at[pl.ds(base + 144 + y * 36, 36)]
    copies = []
    for k in range(3):
        copies.append(send(first, first, sems, 33 + k, xs[k]))
        copies.append(send(second, second, sems, 36 + k, ys[k]))
    wait(copies)
    first = out_ref.at[pl.ds(base, 288)]
    send(first, first, sems, 39, across).wait()


def kernel(count, hidden, weight, partner, whitened, grad_weight, grad_hidden,
           tile, tile_got, tile_sems,
           cent, packed, summed, acc, got_c, got_1, acc_1, got_2, acc_2, got_z, full_z, sems_1, sems_2,
           inv, inv_block, inv_row, white, grad, mirror, total, grad_z,
           strip, away, w_got_c, acc_a, acc_b, w_got_1, w_acc_1, w_got_2, w_acc_2, w_got_z, w_sems):
    here = place()
    x, y, z, c = here
    barrier = pltpu.get_barrier_semaphore()
    for k in range(1, NZ * NC):
        own = lax.rem(z * NC + c + k, NZ * NC)
        pl.semaphore_signal(barrier, inc=1, device_id=device(x, y, lax.div(own, NC), lax.rem(own, NC)), device_id_type=MESH)
    for k in range(1, NX * NY):
        own = lax.rem(x * NY + y + k, NX * NY)
        pl.semaphore_signal(barrier, inc=1, device_id=device(lax.div(own, NY), lax.rem(own, NY), z, c), device_id_type=MESH)
    for part in range(4):
        cols = slice(part * 256, part * 256 + 256)
        strip_e = dot16(hidden[...], weight[:, cols])
        cent[:, cols] = strip_e
        sums = jnp.sum(strip_e, axis=0, keepdims=True)
        tile[0, 2 * part : 2 * part + 1, :] = sums[:, :BLK]
        tile[0, 2 * part + 1 : 2 * part + 2, :] = sums[:, BLK:]
    pl.semaphore_wait(barrier, NZ * NC + NX * NY - 2)
    mean = tile_sum(here, tile, tile_got, tile_sems) * (1.0 / count)
    for i in range(8):
        cols = slice(i * BLK, (i + 1) * BLK)
        cent[:, cols] = cent[:, cols] - mean[i : i + 1, :]
    store_lower(packed, cent, cent)
    all_sum(here, packed, summed, acc, got_c, got_1, acc_1, got_2, acc_2, got_z, full_z, sems_1)
    inverse_factor(1.0 / (count - 1), summed, inv, inv_block, inv_row)
    for part in range(4):
        stop = part * 256 + 256
        white[:, stop - 256 : stop] = dots(cent[:, :stop], inv[stop - 256 : stop, :stop], 1, 1)
    wh = white[...]
    whitened[...] = wh.astype(bf16)
    row_norm = jnp.sqrt(jnp.sum(wh * wh, axis=1, keepdims=True) + epsilon)
    unit = wh / row_norm
    pick = (lax.broadcasted_iota(jnp.int32, (256, 256), 0) == partner[...]).astype(f32)
    pick = (pick + pick.T).astype(bf16)
    near = jnp.zeros_like(unit)
    rest = unit
    for _ in range(3):
        term = rest.astype(bf16)
        near = near + dot16(pick, term)
        rest = rest - term.astype(f32)
    grad_unit = 2.0 * (2.0 * unit - near)
    inner_prod = jnp.sum(wh * grad_unit, axis=1, keepdims=True)
    gr = grad_unit / row_norm - wh * (inner_prod / (row_norm * row_norm * row_norm))
    grad[...] = gr
    store_lower(packed, grad, white)
    sums = jnp.sum(gr, axis=0, keepdims=True)
    sub = lax.broadcasted_iota(jnp.int32, (8, BLK), 0)
    lane = lax.broadcasted_iota(jnp.int32, (8, BLK), 1)
    for i in range(8):
        at = 16 * (i * (i + 1) // 2 + i)
        own = jnp.broadcast_to(sums[:, i * BLK : (i + 1) * BLK], (8, BLK))
        swapped = pltpu.roll(own, 64, 1)
        packed[at] = jnp.where(
            (lane >= 64) & (sub == 0), swapped, jnp.where((lane >= 64) & (sub == 1), own, packed[at])
        )
    all_sum(here, packed, summed, acc, got_c, got_1, acc_1, got_2, acc_2, got_z, full_z, sems_2)
    lane = lax.broadcasted_iota(jnp.int32, (1, BLK), 1)
    r = lax.broadcasted_iota(jnp.int32, (BLK, BLK), 0)
    l = lax.broadcasted_iota(jnp.int32, (BLK, BLK), 1)
    scale = 1.0 / (count - 1)
    for i in range(8):
        for j in range(i + 1):
            block = get_block(summed, i, j)
            turned = block.T
            rows, cols = slice(i * BLK, (i + 1) * BLK), slice(j * BLK, (j + 1) * BLK)
            if i == j:
                mirror[rows, cols] = jnp.where(r >= l, block, turned) * scale
                sums = jnp.where(lane < 64, pltpu.roll(block[0:1, :], 64, 1), block[1:2, :])
                total[:, cols] = grad[:, cols] - sums * (1.0 / count)
            else:
                mirror[rows, cols] = block * scale
                mirror[cols, rows] = turned * scale
    for part in range(4):
        cols = slice(part * 256, part * 256 + 256)
        total[:, cols] = total[:, cols] - dots(white[...], mirror[:, cols])
    for part in range(4):
        start = part * 256
        grad_z[:, start : start + 256] = dots(total[:, start:], inv[start:, start : start + 256]).astype(bf16)
    across = device(x, y, z, 1 - c)
    xs = [device(lax.rem(x + k, NX), y, z, c) for k in range(1, NX)]
    ys = [device(x, lax.rem(y + k, NY), z, c) for k in range(1, NY)]
    zs = [device(x, y, lax.rem(z + k, NZ), c) for k in range(1, NZ)]
    copies = []
    for i in range(4):
        def strips(j, carry):
            own = span(i * 512 + j * BLK, BLK)
            strip[...] = dot16(hidden[:, own], grad_z[...], 0, 0).reshape(NZ, NC, 8, 1024)
            away[i, j] = strip[:, 1 - c]
            keep = strip[:, c]
            acc_a[i, j] = keep[:, :, :512]
            acc_b[j, i] = keep[:, :, 512:]
            return carry

        lax.fori_loop(0, 4, strips, 0)
        copies.append(send(away.at[i], w_got_c.at[i], w_sems, i, across))
    for i in range(4):
        copies[i].wait()

        def add_core(j, carry):
            acc_a[i, j] = acc_a[i, j] + w_got_c[i, j, :, :, :512]
            acc_b[j, i] = acc_b[j, i] + w_got_c[i, j, :, :, 512:]
            return carry

        lax.fori_loop(0, 4, add_core, 0)
    copies = []
    for k in range(3):
        copies.append(send(acc_a.at[lax.rem(x + k + 1, NX)], w_got_1.at[0, k], w_sems, 4 + k, xs[k]))
        copies.append(send(acc_b.at[lax.rem(y + k + 1, NY)], w_got_1.at[1, k], w_sems, 7 + k, ys[k]))

    def hidden_part(k, carry):
        own = span(k * 256, 256)
        grad_hidden[:, own] = dot16(grad_z[...], weight[own, :], 1, 1).astype(bf16)
        return carry

    lax.fori_loop(0, 8, hidden_part, 0)
    wait(copies)

    def add_first(j, carry):
        w_acc_1[0, j] = acc_a[x, j] + w_got_1[0, 0, j] + w_got_1[0, 1, j] + w_got_1[0, 2, j]
        w_acc_1[1, j] = acc_b[y, j] + w_got_1[1, 0, j] + w_got_1[1, 1, j] + w_got_1[1, 2, j]
        return carry

    lax.fori_loop(0, 4, add_first, 0)
    copies = []
    for k in range(3):
        copies.append(send(w_acc_1.at[0, lax.rem(y + k + 1, NY)], w_got_2.at[0, k], w_sems, 10 + k, ys[k]))
        copies.append(send(w_acc_1.at[1, lax.rem(x + k + 1, NX)], w_got_2.at[1, k], w_sems, 13 + k, xs[k]))
    wait(copies)
    w_acc_2[:, 0] = w_acc_1[0, y] + w_got_2[0, 0] + w_got_2[0, 1] + w_got_2[0, 2]
    w_acc_2[:, 1] = w_acc_1[1, x] + w_got_2[1, 0] + w_got_2[1, 1] + w_got_2[1, 2]
    wait([send(w_acc_2.at[lax.rem(z + k + 1, NZ)], w_got_z.at[k], w_sems, 16 + k, zs[k]) for k in range(7)])
    own = w_acc_2[z]
    for k in range(7):
        own = own + w_got_z[k]
    grad_weight[:, :512] = own[0]
    grad_weight[:, 512:] = own[1]


def body(hidden, weight, partners):
    count = hidden.shape[0] * lax.axis_size("group") * lax.axis_size("dp")
    vmem = pl.BlockSpec(memory_space=pltpu.VMEM)
    V, sem = pltpu.VMEM, pltpu.SemaphoreType.DMA
    return pl.pallas_call(
        functools.partial(kernel, count),
        out_shape=(
            jax.ShapeDtypeStruct((256, 1024), bf16),
            jax.ShapeDtypeStruct((8, 1024), f32),
            jax.ShapeDtypeStruct((256, 2048), bf16),
        ),
        in_specs=[vmem] * 3,
        out_specs=(vmem,) * 3,
        scratch_shapes=[
            V((2, 8, 128), f32), V((2, 15, 8, 128), f32), sem((2, 30)),
            V((256, 1024), f32), V((576, 8, 128), f32), V((576, 8, 128), f32),
            V((288, 8, 128), f32), V((288, 8, 128), f32), V((2, 3, 36, 8, 128), f32), V((2, 36, 8, 128), f32),
            V((2, 3, T, 8, 128), f32), V((24, 8, 128), f32), V((7, 3, 8, 128), f32), V((24, 8, 128), f32),
            sem((2, 40)), sem((2, 40)),
            V((1024, 1024), f32), V((BLK, BLK), f32), V((BLK, 1024), f32), V((256, 1024), f32),
            V((256, 1024), f32), V((1024, 1024), f32), V((256, 1024), f32), V((256, 1024), bf16),
            V((8, 2, 8, 1024), f32), V((4, 4, 8, 8, 1024), f32), V((4, 4, 8, 8, 1024), f32),
            V((4, 4, 8, 8, 512), f32), V((4, 4, 8, 8, 512), f32), V((2, 3, 4, 8, 8, 512), f32),
            V((2, 4, 8, 8, 512), f32), V((2, 3, 8, 8, 512), f32), V((8, 2, 8, 512), f32), V((7, 2, 8, 512), f32),
            sem((2, 23)),
        ],
        compiler_params=pltpu.CompilerParams(collective_id=0, has_side_effects=True, vmem_limit_bytes=60 * MB),
        name="whitening_step",
    )(hidden, weight, partners)


def solution(mesh):
    return jax.shard_map(
        body,
        mesh=mesh,
        in_specs=(P(("group", "dp"), None), P(), P(("group", "dp"), None)),
        out_specs=(P(("group", "dp"), None), P(("group", "dp"), None), P(("group", "dp"), None)),
        check_vma=False,
    )
```

time: 2480 us -> 243 us (0.10)
  waiting for transfers between devices: 1790 us -> 0 us
  other arithmetic: 275 us -> 0 us
  Pallas kernels: 0 us -> 235 us
  blocking collectives: 155 us -> 0 us
  matrix products: 136 us -> 0 us
  local copies, waits for them, and re-layouts: 96.8 us -> 5.55 us
    unnamed x4 -> x0, waiting for transfers between devices: 1270 us -> none
    psum x2 -> x0, waiting for transfers between devices: 521 us -> none  [the longest x1 262 us: body(): lax.psum(jnp.dot(centered.T, centered, precision=highest), ('group', 'dp'))]
    another operation x33 -> x0, other arithmetic: 257 us -> none  [the longest x30 172 us: body(): factor = jnp.linalg.cholesky(cov)]
    pallas_call x0 -> x1, Pallas kernels: none -> 235 us  [body(): pl.pallas_call(functools.partial(kernel, count), out_shape=(jax.ShapeDtyp...]
    psum x2 -> x0, blocking collectives: 155 us -> none  [the longest x1 79.1 us: body(): mean_row = lax.psum(jnp.sum(embedded, axis=0), ('group', 'dp')) / total_rows]
    another operation x74 -> x0, matrix products: 102 us -> none  [the longest x15 30.5 us: body(): lax.linalg.triangular_solve(factor, left_solved, left_side=False, lower=T...]
    another operation x46 -> x0, local copies, waits for them, and re-layouts: 37.7 us -> none
    dot_general x6 -> x0, matrix products: 33.3 us -> none  [the longest x1 10 us: body(): jnp.dot(centered, grad_cov, precision=highest)]
  transfers between devices with their start and end apart: 3 -> 0, of which waited for: 3 -> 0; matrix products, arithmetic and copies ran while one was open for 1% -> 0% of each run, Pallas kernels for 0% -> 0%
where the time goes in v3:
time: 243 us; the launch traced here: 241 us
  Pallas kernels  235 us (97%)
  local copies, waits for them, and re-layouts  5.55 us (2%)
    pallas_call x1, Pallas kernels, body(): pl.pallas_call(functools.partial(kernel, count), out_shape=(jax.ShapeDtyp...  235 us
    unnamed x3, local copies, waits for them, and re-layouts  5.55 us

profile of v3, /device:TPU:0, one launch (start us, length us, event | category | flops | bytes accessed | tf_op | source)
XLA Modules:
  0.0 241.2 jit_solution(12324868759234749235)
XLA Ops:
  0.6 235.0 %whitening_step.1 = (bf16[256,1024]{1,0:T(8,128)(2,1)}, f32[8,1024]{1,0:T(8,128)}, bf16[256,2048]{1,0:T(8,128)(2,1)}) custom-call(bf16[256,2048]{1,0:T(8,128)(2,1)} %hidden.1, bf16[2048,1024]{1,0:T(8,128)(2,1)} %weight.1, s32[1,256]{1,0:T(1,128)} %partner.1), custom_call_target="tpu_custom_call" | custom-call | tf_op jit(solution)/shard_map/whitening_step/pallas_call | solution.py:396
  235.7 1.9 copy.9
  237.5 1.4 copy.10
  238.9 2.3 copy.11

commit v4 on v3

--- a/solution.py
+++ b/solution.py
@@ -26,8 +26,8 @@
     return (x, (y * NZ + z) * NC + c)
 
 
-def send(src, dst, sems, slot, peer):
-    copy = pltpu.make_async_remote_copy(
+def remote(src, dst, sems, slot, peer):
+    return pltpu.make_async_remote_copy(
         src_ref=src,
         dst_ref=dst,
         send_sem=sems.at[0, slot],
@@ -35,13 +35,26 @@
         device_id=peer,
         device_id_type=MESH,
     )
-    copy.start()
-    return copy
+
+
+def start(copies):
+    for copy in copies:
+        copy.start()
 
 
 def wait(copies):
     for copy in copies:
         copy.wait()
+
+
+def send(src, dst, sems, slot, peer):
+    copy = remote(src, dst, sems, slot, peer)
+    copy.start()
+    return copy
+
+
+def nothing():
+    pass
 
 
 def dots(a, b, ca=1, cb=0):
@@ -116,7 +129,7 @@
     return [jnp.where(lane <= sub + 8 * p, pan[p], 0.0) for p in range(16)]
 
 
-def inverse_factor(scale, in_ref, out_ref, inv_ref, row_ref):
+def inverse_factor(scale, in_ref, out_ref, inv_ref, row_ref, beside):
     for i in range(8):
         for j in range(i + 1):
             block = get_block(in_ref, i, j) * scale
@@ -132,6 +145,8 @@
     lane = lax.broadcasted_iota(jnp.int32, (BLK, 1024), 1)
 
     def step(i, carry):
+        for at, work in beside.items():
+            pl.when(i == at)(work)
         own = span(i * BLK, BLK)
         pans = [out_ref[span(i * BLK + 8 * p, 8), own] for p in range(16)]
         for p, tile in enumerate(inverse_factor_block(pans)):
@@ -189,13 +204,13 @@
     wait(copies)
     for k in range(15):
         total = total + got[1, k]
-    return total
+    tile[2] = total
 
 
 T = 9
 
 
-def all_sum(here, in_ref, out_ref, acc, got_c, got_1, acc_1, got_2, acc_2, got_z, full_z, sems):
+def all_sum(here, in_ref, out_ref, acc, got_c, got_1, acc_1, got_2, acc_2, got_z, full_z, sems, during, after):
     x, y, z, c = here
     across = device(x, y, z, 1 - c)
     xs = [device(lax.rem(x + k, NX), y, z, c) for k in range(1, NX)]
@@ -204,13 +219,18 @@
     x_at = [lax.rem(x + k, NX) for k in range(1, NX)]
     y_at = [lax.rem(y + k, NY) for k in range(1, NY)]
     z_at = [lax.rem(z + k, NZ) for k in range(1, NZ)]
-    send(in_ref.at[pl.ds((1 - c) * 288, 288)], got_c, sems, 0, across).wait()
+    copy = send(in_ref.at[pl.ds((1 - c) * 288, 288)], got_c, sems, 0, across)
+    during.get("core", nothing)()
+    copy.wait()
+    after.get("core", nothing)()
     acc[...] = in_ref[pl.ds(c * 288, 288)] + got_c[...]
     copies = []
     for k in range(3):
         copies.append(send(acc.at[pl.ds(x_at[k] * 36, 36)], got_1.at[0, k], sems, 1 + k, xs[k]))
         copies.append(send(acc.at[pl.ds(144 + y_at[k] * 36, 36)], got_1.at[1, k], sems, 4 + k, ys[k]))
+    during.get("first", nothing)()
     wait(copies)
+    after.get("first", nothing)()
     acc_1[0] = acc[pl.ds(x * 36, 36)] + got_1[0, 0] + got_1[0, 1] + got_1[0, 2]
     acc_1[1] = acc[pl.ds(144 + y * 36, 36)] + got_1[1, 0] + got_1[1, 1] + got_1[1, 2]
     copies = []
@@ -244,16 +264,127 @@
         copies.append(send(second, second, sems, 36 + k, ys[k]))
     wait(copies)
     first = out_ref.at[pl.ds(base, 288)]
-    send(first, first, sems, 39, across).wait()
+    copy = send(first, first, sems, 39, across)
+    during.get("core back", nothing)()
+    copy.wait()
+
+
+class RowScatter:
+    def __init__(self, here, hidden, high, low, strip, away, got_c, acc_a, acc_b, got_1, acc_1, got_2, acc_2, got_z, sems):
+        self.here, self.hidden, self.high, self.low, self.strip, self.away = here, hidden, high, low, strip, away
+        self.got_c, self.acc_a, self.acc_b, self.got_1, self.acc_1 = got_c, acc_a, acc_b, got_1, acc_1
+        self.got_2, self.acc_2, self.got_z, self.sems = got_2, acc_2, got_z, sems
+
+    def strips(self):
+        c = self.here[3]
+
+        def one(k, carry):
+            i, j = lax.div(k, 4), lax.rem(k, 4)
+            own = self.hidden[:, span(k * BLK, BLK)]
+            both = dot16(own, self.high[...], 0, 0) + dot16(own, self.low[...], 0, 0)
+            self.strip[...] = both.reshape(NZ, NC, 8, 1024)
+            self.away[i, j] = self.strip[:, 1 - c]
+            keep = self.strip[:, c]
+            self.acc_a[i, j] = keep[:, :, :512]
+            self.acc_b[j, i] = keep[:, :, 512:]
+            return carry
+
+        lax.fori_loop(0, 16, one, 0)
+
+    def core(self):
+        x, y, z, c = self.here
+        return [remote(self.away, self.got_c, self.sems, 0, device(x, y, z, 1 - c))]
+
+    def core_start(self):
+        start(self.core())
+
+    def core_end(self):
+        wait(self.core())
+
+        def add(k, carry):
+            i, j = lax.div(k, 4), lax.rem(k, 4)
+            self.acc_a[i, j] = self.acc_a[i, j] + self.got_c[i, j, :, :, :512]
+            self.acc_b[j, i] = self.acc_b[j, i] + self.got_c[i, j, :, :, 512:]
+            return carry
+
+        lax.fori_loop(0, 16, add, 0)
+
+    def first(self):
+        x, y, z, c = self.here
+        copies = []
+        for k in range(3):
+            xk, yk = lax.rem(x + k + 1, NX), lax.rem(y + k + 1, NY)
+            copies.append(remote(self.acc_a.at[xk], self.got_1.at[0, k], self.sems, 4 + k, device(xk, y, z, c)))
+            copies.append(remote(self.acc_b.at[yk], self.got_1.at[1, k], self.sems, 7 + k, device(x, yk, z, c)))
+        return copies
+
+    def first_start(self):
+        start(self.first())
+
+    def first_end(self):
+        x, y, z, c = self.here
+        wait(self.first())
+        got = self.got_1
+
+        def add(j, carry):
+            self.acc_1[0, j] = self.acc_a[x, j] + got[0, 0, j] + got[0, 1, j] + got[0, 2, j]
+            self.acc_1[1, j] = self.acc_b[y, j] + got[1, 0, j] + got[1, 1, j] + got[1, 2, j]
+            return carry
+
+        lax.fori_loop(0, 4, add, 0)
+
+    def second(self):
+        x, y, z, c = self.here
+        copies = []
+        for k in range(3):
+            xk, yk = lax.rem(x + k + 1, NX), lax.rem(y + k + 1, NY)
+            copies.append(remote(self.acc_1.at[0, yk], self.got_2.at[0, k], self.sems, 10 + k, device(x, yk, z, c)))
+            copies.append(remote(self.acc_1.at[1, xk], self.got_2.at[1, k], self.sems, 13 + k, device(xk, y, z, c)))
+        return copies
+
+    def second_start(self):
+        start(self.second())
+
+    def second_end(self):
+        x, y, z, c = self.here
+        wait(self.second())
+        got = self.got_2
+        self.acc_2[:, 0] = self.acc_1[0, y] + got[0, 0] + got[0, 1] + got[0, 2]
+        self.acc_2[:, 1] = self.acc_1[1, x] + got[1, 0] + got[1, 1] + got[1, 2]
+
+    def third(self):
+        x, y, z, c = self.here
+        copies = []
+        for k in range(7):
+            zk = lax.rem(z + k + 1, NZ)
+            copies.append(remote(self.acc_2.at[zk], self.got_z.at[k], self.sems, 16 + k, device(x, y, zk, c)))
+        return copies
+
+    def third_start(self):
+        start(self.third())
+
+    def third_end(self, out_ref, row):
+        wait(self.third())
+        own = self.acc_2[self.here[2]]
+        for k in range(7):
+            own = own + self.got_z[k]
+        out_ref[row : row + 8, :512] = own[0]
+        out_ref[row : row + 8, 512:] = own[1]
+
+
+def split(rows, high, low):
+    high[...] = rows.astype(bf16)
+    low[...] = (rows - high[...].astype(f32)).astype(bf16)
 
 
 def kernel(count, hidden, weight, partner, whitened, grad_weight, grad_hidden,
            tile, tile_got, tile_sems,
            cent, packed, summed, acc, got_c, got_1, acc_1, got_2, acc_2, got_z, full_z, sems_1, sems_2,
-           inv, inv_block, inv_row, white, grad, mirror, total, grad_z,
-           strip, away, w_got_c, acc_a, acc_b, w_got_1, w_acc_1, w_got_2, w_acc_2, w_got_z, w_sems):
+           inv, inv_block, inv_row, white, grad, mirror, total, grad_z, grad_mean, late, high, low,
+           strip, away, w_got_c, acc_a, acc_b, w_got_1, w_acc_1, w_got_2, w_acc_2, w_got_z, w_sems_1, w_sems_2):
     here = place()
     x, y, z, c = here
+    N = 256
     barrier = pltpu.get_barrier_semaphore()
     for k in range(1, NZ * NC):
         own = lax.rem(z * NC + c + k, NZ * NC)
@@ -264,26 +395,50 @@
     for part in range(4):
         cols = slice(part * 256, part * 256 + 256)
         strip_e = dot16(hidden[...], weight[:, cols])
-        cent[:, cols] = strip_e
+        cent[:N, cols] = strip_e
         sums = jnp.sum(strip_e, axis=0, keepdims=True)
         tile[0, 2 * part : 2 * part + 1, :] = sums[:, :BLK]
         tile[0, 2 * part + 1 : 2 * part + 2, :] = sums[:, BLK:]
+    sums = dot16(jnp.ones((8, N), bf16), hidden[...])
+    for i in range(16):
+        tile[0, 8 + i : 9 + i, :] = sums[0:1, i * BLK : (i + 1) * BLK]
     pl.semaphore_wait(barrier, NZ * NC + NX * NY - 2)
-    mean = tile_sum(here, tile, tile_got, tile_sems) * (1.0 / count)
+    tile_sum(here, tile, tile_got, tile_sems)
     for i in range(8):
         cols = slice(i * BLK, (i + 1) * BLK)
-        cent[:, cols] = cent[:, cols] - mean[i : i + 1, :]
-    store_lower(packed, cent, cent)
-    all_sum(here, packed, summed, acc, got_c, got_1, acc_1, got_2, acc_2, got_z, full_z, sems_1)
-    inverse_factor(1.0 / (count - 1), summed, inv, inv_block, inv_row)
+        cent[:N, cols] = cent[:N, cols] - tile[2, i : i + 1, :] * (1.0 / count)
+    store_lower(packed, cent[:N, :], cent[:N, :])
+    split(cent[:N, :], high, low)
+    reduce_buffers = (acc, got_c, got_1, acc_1, got_2, acc_2, got_z, full_z)
+    row_buffers = (high, low, strip, away, w_got_c, acc_a, acc_b, w_got_1, w_acc_1, w_got_2, w_acc_2, w_got_z)
+    by_cent = RowScatter(here, hidden, *row_buffers, w_sems_1)
+    by_grad = RowScatter(here, hidden, *row_buffers, w_sems_2)
+
+    def cent_strips():
+        by_cent.strips()
+        by_cent.core_start()
+
+    all_sum(here, packed, summed, *reduce_buffers, sems_1, {"first": cent_strips, "core back": by_cent.core_end}, {})
+    by_cent.first_start()
+
+    def to_second():
+        by_cent.first_end()
+        by_cent.second_start()
+
+    def to_third():
+        by_cent.second_end()
+        by_cent.third_start()
+
+    inverse_factor(1.0 / (count - 1), summed, inv, inv_block, inv_row, {4: to_second, 6: to_third})
+    by_cent.third_end(cent, N)
     for part in range(4):
         stop = part * 256 + 256
         white[:, stop - 256 : stop] = dots(cent[:, :stop], inv[stop - 256 : stop, :stop], 1, 1)
-    wh = white[...]
+    wh = white[:N, :]
     whitened[...] = wh.astype(bf16)
     row_norm = jnp.sqrt(jnp.sum(wh * wh, axis=1, keepdims=True) + epsilon)
     unit = wh / row_norm
-    pick = (lax.broadcasted_iota(jnp.int32, (256, 256), 0) == partner[...]).astype(f32)
+    pick = (lax.broadcasted_iota(jnp.int32, (N, N), 0) == partner[...]).astype(f32)
     pick = (pick + pick.T).astype(bf16)
     near = jnp.zeros_like(unit)
     rest = unit
@@ -295,7 +450,8 @@
     inner_prod = jnp.sum(wh * grad_unit, axis=1, keepdims=True)
     gr = grad_unit / row_norm - wh * (inner_prod / (row_norm * row_norm * row_norm))
     grad[...] = gr
-    store_lower(packed, grad, white)
+    split(gr, high, low)
+    store_lower(packed, grad[...], white[:N, :])
     sums = jnp.sum(gr, axis=0, keepdims=True)
     sub = lax.broadcasted_iota(jnp.int32, (8, BLK), 0)
     lane = lax.broadcasted_iota(jnp.int32, (8, BLK), 1)
@@ -306,8 +462,12 @@
         packed[at] = jnp.where(
             (lane >= 64) & (sub == 0), swapped, jnp.where((lane >= 64) & (sub == 1), own, packed[at])
         )
-    all_sum(here, packed, summed, acc, got_c, got_1, acc_1, got_2, acc_2, got_z, full_z, sems_2)
-    lane = lax.broadcasted_iota(jnp.int32, (1, BLK), 1)
+    all_sum(
+        here, packed, summed, *reduce_buffers, sems_2,
+        {"core": by_grad.strips, "first": by_grad.core_end},
+        {"core": by_grad.core_start, "first": by_grad.first_start},
+    )
+    lane1 = lax.broadcasted_iota(jnp.int32, (1, BLK), 1)
     r = lax.broadcasted_iota(jnp.int32, (BLK, BLK), 0)
     l = lax.broadcasted_iota(jnp.int32, (BLK, BLK), 1)
     scale = 1.0 / (count - 1)
@@ -318,75 +478,38 @@
             rows, cols = slice(i * BLK, (i + 1) * BLK), slice(j * BLK, (j + 1) * BLK)
             if i == j:
                 mirror[rows, cols] = jnp.where(r >= l, block, turned) * scale
-                sums = jnp.where(lane < 64, pltpu.roll(block[0:1, :], 64, 1), block[1:2, :])
-                total[:, cols] = grad[:, cols] - sums * (1.0 / count)
+                sums = jnp.where(lane1 < 64, pltpu.roll(block[0:1, :], 64, 1), block[1:2, :]) * (1.0 / count)
+                grad_mean[:, cols] = jnp.broadcast_to(sums, (8, BLK))
+                total[:N, cols] = grad[:, cols] - sums
             else:
                 mirror[rows, cols] = block * scale
                 mirror[cols, rows] = turned * scale
+    total[N:, :] = jnp.zeros((8, 1024), f32)
     for part in range(4):
         cols = slice(part * 256, part * 256 + 256)
         total[:, cols] = total[:, cols] - dots(white[...], mirror[:, cols])
     for part in range(4):
-        start = part * 256
-        grad_z[:, start : start + 256] = dots(total[:, start:], inv[start:, start : start + 256]).astype(bf16)
-    across = device(x, y, z, 1 - c)
-    xs = [device(lax.rem(x + k, NX), y, z, c) for k in range(1, NX)]
-    ys = [device(x, lax.rem(y + k, NY), z, c) for k in range(1, NY)]
-    zs = [device(x, y, lax.rem(z + k, NZ), c) for k in range(1, NZ)]
-    copies = []
-    for i in range(4):
-        def strips(j, carry):
-            own = span(i * 512 + j * BLK, BLK)
-            strip[...] = dot16(hidden[:, own], grad_z[...], 0, 0).reshape(NZ, NC, 8, 1024)
-            away[i, j] = strip[:, 1 - c]
-            keep = strip[:, c]
-            acc_a[i, j] = keep[:, :, :512]
-            acc_b[j, i] = keep[:, :, 512:]
-            return carry
-
-        lax.fori_loop(0, 4, strips, 0)
-        copies.append(send(away.at[i], w_got_c.at[i], w_sems, i, across))
-    for i in range(4):
-        copies[i].wait()
-
-        def add_core(j, carry):
-            acc_a[i, j] = acc_a[i, j] + w_got_c[i, j, :, :, :512]
-            acc_b[j, i] = acc_b[j, i] + w_got_c[i, j, :, :, 512:]
-            return carry
-
-        lax.fori_loop(0, 4, add_core, 0)
-    copies = []
-    for k in range(3):
-        copies.append(send(acc_a.at[lax.rem(x + k + 1, NX)], w_got_1.at[0, k], w_sems, 4 + k, xs[k]))
-        copies.append(send(acc_b.at[lax.rem(y + k + 1, NY)], w_got_1.at[1, k], w_sems, 7 + k, ys[k]))
+        start_at = part * 256
+        cols = slice(start_at, start_at + 256)
+        both = dots(total[:, start_at:], inv[start_at:, cols])
+        grad_z[:, cols] = both[:N].astype(bf16)
+        late[:, cols] = both[N:]
 
     def hidden_part(k, carry):
         own = span(k * 256, 256)
         grad_hidden[:, own] = dot16(grad_z[...], weight[own, :], 1, 1).astype(bf16)
         return carry
 
+    by_grad.first_end()
+    by_grad.second_start()
     lax.fori_loop(0, 8, hidden_part, 0)
-    wait(copies)
-
-    def add_first(j, carry):
-        w_acc_1[0, j] = acc_a[x, j] + w_got_1[0, 0, j] + w_got_1[0, 1, j] + w_got_1[0, 2, j]
-        w_acc_1[1, j] = acc_b[y, j] + w_got_1[1, 0, j] + w_got_1[1, 1, j] + w_got_1[1, 2, j]
-        return carry
-
-    lax.fori_loop(0, 4, add_first, 0)
-    copies = []
-    for k in range(3):
-        copies.append(send(w_acc_1.at[0, lax.rem(y + k + 1, NY)], w_got_2.at[0, k], w_sems, 10 + k, ys[k]))
-        copies.append(send(w_acc_1.at[1, lax.rem(x + k + 1, NX)], w_got_2.at[1, k], w_sems, 13 + k, xs[k]))
-    wait(copies)
-    w_acc_2[:, 0] = w_acc_1[0, y] + w_got_2[0, 0] + w_got_2[0, 1] + w_got_2[0, 2]
-    w_acc_2[:, 1] = w_acc_1[1, x] + w_got_2[1, 0] + w_got_2[1, 1] + w_got_2[1, 2]
-    wait([send(w_acc_2.at[lax.rem(z + k + 1, NZ)], w_got_z.at[k], w_sems, 16 + k, zs[k]) for k in range(7)])
-    own = w_acc_2[z]
-    for k in range(7):
-        own = own + w_got_z[k]
-    grad_weight[:, :512] = own[0]
-    grad_weight[:, 512:] = own[1]
+    by_grad.second_end()
+    by_grad.third_start()
+    units = jnp.broadcast_to(tile[2, pl.ds(8 + x * NY + y, 1), :], (8, BLK))
+    mine = jnp.sum(jnp.where(lane == (z * NC + c) * 8 + sub, units, 0.0), axis=1, keepdims=True)
+    by_grad.third_end(total, N)
+    rows = total[N:, :] - mine * grad_mean[...]
+    grad_weight[...] = late[...] + dots(rows, inv[...])
 
 
 def body(hidden, weight, partners):
@@ -403,17 +526,18 @@
         in_specs=[vmem] * 3,
         out_specs=(vmem,) * 3,
         scratch_shapes=[
-            V((2, 8, 128), f32), V((2, 15, 8, 128), f32), sem((2, 30)),
-            V((256, 1024), f32), V((576, 8, 128), f32), V((576, 8, 128), f32),
+            V((3, 24, 128), f32), V((2, 15, 24, 128), f32), sem((2, 30)),
+            V((264, 1024), f32), V((576, 8, 128), f32), V((576, 8, 128), f32),
             V((288, 8, 128), f32), V((288, 8, 128), f32), V((2, 3, 36, 8, 128), f32), V((2, 36, 8, 128), f32),
             V((2, 3, T, 8, 128), f32), V((24, 8, 128), f32), V((7, 3, 8, 128), f32), V((24, 8, 128), f32),
             sem((2, 40)), sem((2, 40)),
-            V((1024, 1024), f32), V((BLK, BLK), f32), V((BLK, 1024), f32), V((256, 1024), f32),
-            V((256, 1024), f32), V((1024, 1024), f32), V((256, 1024), f32), V((256, 1024), bf16),
+            V((1024, 1024), f32), V((BLK, BLK), f32), V((BLK, 1024), f32), V((264, 1024), f32),
+            V((256, 1024), f32), V((1024, 1024), f32), V((264, 1024), f32), V((256, 1024), bf16),
+            V((8, 1024), f32), V((8, 1024), f32), V((256, 1024), bf16), V((256, 1024), bf16),
             V((8, 2, 8, 1024), f32), V((4, 4, 8, 8, 1024), f32), V((4, 4, 8, 8, 1024), f32),
             V((4, 4, 8, 8, 512), f32), V((4, 4, 8, 8, 512), f32), V((2, 3, 4, 8, 8, 512), f32),
             V((2, 4, 8, 8, 512), f32), V((2, 3, 8, 8, 512), f32), V((8, 2, 8, 512), f32), V((7, 2, 8, 512), f32),
-            sem((2, 23)),
+            sem((2, 23)), sem((2, 23)),
         ],
         compiler_params=pltpu.CompilerParams(collective_id=0, has_side_effects=True, vmem_limit_bytes=60 * MB),
         name="whitening_step",

time: 243 us -> 246 us (1.012)
  Pallas kernels: 235 us -> 238 us
    pallas_call x1, Pallas kernels: 235 us -> 238 us  [body(): pl.pallas_call(functools.partial(kernel, count), out_shape=(jax.ShapeDtyp...]
where the time goes in v4:
time: 246 us; the launch traced here: 244 us
  Pallas kernels  238 us (97%)
  local copies, waits for them, and re-layouts  5.55 us (2%)
    pallas_call x1, Pallas kernels, body(): pl.pallas_call(functools.partial(kernel, count), out_shape=(jax.ShapeDtyp...  238 us
    unnamed x3, local copies, waits for them, and re-layouts  5.55 us

profile of v4, /device:TPU:0, one launch (start us, length us, event | category | flops | bytes accessed | tf_op | source)
XLA Modules:
  0.0 244.1 jit_solution(5750735142007777576)
XLA Ops:
  0.6 237.9 %whitening_step.1 = (bf16[256,1024]{1,0:T(8,128)(2,1)}, f32[8,1024]{1,0:T(8,128)}, bf16[256,2048]{1,0:T(8,128)(2,1)}) custom-call(bf16[256,2048]{1,0:T(8,128)(2,1)} %hidden.1, bf16[2048,1024]{1,0:T(8,128)(2,1)} %weight.1, s32[1,256]{1,0:T(1,128)} %partner.1), custom_call_target="tpu_custom_call" | custom-call | tf_op jit(solution)/shard_map/whitening_step/pallas_call | solution.py:519
  238.5 1.9 copy.9
  240.4 1.4 copy.10
  241.8 2.3 copy.11

commit v5 on v4

--- a/solution.py
+++ b/solution.py
@@ -210,7 +210,7 @@
 T = 9
 
 
-def all_sum(here, in_ref, out_ref, acc, got_c, got_1, acc_1, got_2, acc_2, got_z, full_z, sems, during, after):
+def all_sum(here, in_ref, out_ref, acc, got_c, got_1, acc_1, got_2, acc_2, got_z, full_z, sems, during):
     x, y, z, c = here
     across = device(x, y, z, 1 - c)
     xs = [device(lax.rem(x + k, NX), y, z, c) for k in range(1, NX)]
@@ -222,7 +222,6 @@
     copy = send(in_ref.at[pl.ds((1 - c) * 288, 288)], got_c, sems, 0, across)
     during.get("core", nothing)()
     copy.wait()
-    after.get("core", nothing)()
     acc[...] = in_ref[pl.ds(c * 288, 288)] + got_c[...]
     copies = []
     for k in range(3):
@@ -230,24 +229,28 @@
         copies.append(send(acc.at[pl.ds(144 + y_at[k] * 36, 36)], got_1.at[1, k], sems, 4 + k, ys[k]))
     during.get("first", nothing)()
     wait(copies)
-    after.get("first", nothing)()
     acc_1[0] = acc[pl.ds(x * 36, 36)] + got_1[0, 0] + got_1[0, 1] + got_1[0, 2]
     acc_1[1] = acc[pl.ds(144 + y * 36, 36)] + got_1[1, 0] + got_1[1, 1] + got_1[1, 2]
     copies = []
     for k in range(3):
         copies.append(send(acc_1.at[0, pl.ds(y_at[k] * T, T)], got_2.at[0, k], sems, 7 + k, ys[k]))
         copies.append(send(acc_1.at[1, pl.ds(x_at[k] * T, T)], got_2.at[1, k], sems, 10 + k, xs[k]))
+    during.get("second", nothing)()
     wait(copies)
     acc_2[0:T] = acc_1[0, pl.ds(y * T, T)] + got_2[0, 0] + got_2[0, 1] + got_2[0, 2]
     acc_2[T : 2 * T] = acc_1[1, pl.ds(x * T, T)] + got_2[1, 0] + got_2[1, 1] + got_2[1, 2]
     acc_2[2 * T : 24] = jnp.zeros((24 - 2 * T, 8, 128), f32)
-    wait([send(acc_2.at[pl.ds(3 * z_at[k], 3)], got_z.at[k], sems, 13 + k, zs[k]) for k in range(7)])
+    copies = [send(acc_2.at[pl.ds(3 * z_at[k], 3)], got_z.at[k], sems, 13 + k, zs[k]) for k in range(7)]
+    during.get("third", nothing)()
+    wait(copies)
     own = acc_2[pl.ds(3 * z, 3)]
     for k in range(7):
         own = own + got_z[k]
     mine = full_z.at[pl.ds(3 * z, 3)]
     mine[...] = own
-    wait([send(mine, mine, sems, 20 + k, zs[k]) for k in range(7)])
+    copies = [send(mine, mine, sems, 20 + k, zs[k]) for k in range(7)]
+    during.get("third back", nothing)()
+    wait(copies)
     base = c * 288
     first, second = out_ref.at[pl.ds(base + (x * 4 + y) * T, T)], out_ref.at[pl.ds(base + 144 + (y * 4 + x) * T, T)]
     first[...] = full_z[0:T]
@@ -280,8 +283,8 @@
 
         def one(k, carry):
             i, j = lax.div(k, 4), lax.rem(k, 4)
-            own = self.hidden[:, span(k * BLK, BLK)]
-            both = dot16(own, self.high[...], 0, 0) + dot16(own, self.low[...], 0, 0)
+            own = self.hidden[span(k * BLK, BLK), :]
+            both = dot16(own, self.high[...]) + dot16(own, self.low[...])
             self.strip[...] = both.reshape(NZ, NC, 8, 1024)
             self.away[i, j] = self.strip[:, 1 - c]
             keep = self.strip[:, c]
@@ -309,37 +312,67 @@
 
         lax.fori_loop(0, 16, add, 0)
 
-    def first(self):
+    def ring(self, slots):
+        x, y, z, c = self.here
+        copies = []
+        for axis, at, size, acc in ((0, x, NX, self.acc_a), (1, y, NY, self.acc_b)):
+            up, far, down = lax.rem(at + 1, size), lax.rem(at + 2, size), lax.rem(at + 3, size)
+            plus = device(up, y, z, c) if axis == 0 else device(x, up, z, c)
+            minus = device(down, y, z, c) if axis == 0 else device(x, down, z, c)
+            routes = (
+                (acc.at[far, 0:2], plus),
+                (acc.at[far, 2:4], minus),
+                (acc.at[down, 0:2], minus),
+                (acc.at[up, 2:4], plus),
+                (acc.at[up, 0:2], plus),
+                (acc.at[down, 2:4], minus),
+            )
+            for slot in slots:
+                src, peer = routes[slot]
+                copies.append(remote(src, self.got_1.at[axis, slot], self.sems, 1 + 6 * axis + slot, peer))
+        return copies
+
+    def far_start(self):
+        start(self.ring((0, 1)))
+
+    def near_start(self):
+        start(self.ring((2, 3)))
+
+    def pass_on(self):
+        x, y, z, c = self.here
+        wait(self.ring((0, 1)))
+        for axis, at, size, acc in ((0, x, NX, self.acc_a), (1, y, NY, self.acc_b)):
+            up, down = lax.rem(at + 1, size), lax.rem(at + 3, size)
+
+            def add(j, carry):
+                acc[up, j] = acc[up, j] + self.got_1[axis, 0, j]
+                acc[down, 2 + j] = acc[down, 2 + j] + self.got_1[axis, 1, j]
+                return carry
+
+            lax.fori_loop(0, 2, add, 0)
+        start(self.ring((4, 5)))
+
+    def first_end(self):
+        x, y, z, c = self.here
+        wait(self.ring((2, 3)))
+        wait(self.ring((4, 5)))
+        for axis, at, acc in ((0, x, self.acc_a), (1, y, self.acc_b)):
+            got = self.got_1
+
+            def add(j, carry):
+                self.acc_1[axis, j] = acc[at, j] + got[axis, 2, j] + got[axis, 4, j]
+                self.acc_1[axis, 2 + j] = acc[at, 2 + j] + got[axis, 3, j] + got[axis, 5, j]
+                return carry
+
+            lax.fori_loop(0, 2, add, 0)
+
+    def second(self):
         x, y, z, c = self.here
         copies = []
         for k in range(3):
             xk, yk = lax.rem(x + k + 1, NX), lax.rem(y + k + 1, NY)
-            copies.append(remote(self.acc_a.at[xk], self.got_1.at[0, k], self.sems, 4 + k, device(xk, y, z, c)))
-            copies.append(remote(self.acc_b.at[yk], self.got_1.at[1, k], self.sems, 7 + k, device(x, yk, z, c)))
-        return copies
-
-    def first_start(self):
-        start(self.first())
-
-    def first_end(self):
-        x, y, z, c = self.here
-        wait(self.first())
-        got = self.got_1
-
-        def add(j, carry):
-            self.acc_1[0, j] = self.acc_a[x, j] + got[0, 0, j] + got[0, 1, j] + got[0, 2, j]
-            self.acc_1[1, j] = self.acc_b[y, j] + got[1, 0, j] + got[1, 1, j] + got[1, 2, j]
-            return carry
-
-        lax.fori_loop(0, 4, add, 0)
-
-    def second(self):
-        x, y, z, c = self.here
-        copies = []
-        for k in range(3):
-            xk, yk = lax.rem(x + k + 1, NX), lax.rem(y + k + 1, NY)
-            copies.append(remote(self.acc_1.at[0, yk], self.got_2.at[0, k], self.sems, 10 + k, device(x, yk, z, c)))
-            copies.append(remote(self.acc_1.at[1, xk], self.got_2.at[1, k], self.sems, 13 + k, device(xk, y, z, c)))
+            copies.append(remote(self.acc_1.at[0, yk], self.got_2.at[0, k], self.sems, 13 + k, device(x, yk, z, c)))
+            copies.append(remote(self.acc_1.at[1, xk], self.got_2.at[1, k], self.sems, 16 + k, device(xk, y, z, c)))
         return copies
 
     def second_start(self):
@@ -357,7 +390,7 @@
         copies = []
         for k in range(7):
             zk = lax.rem(z + k + 1, NZ)
-            copies.append(remote(self.acc_2.at[zk], self.got_z.at[k], self.sems, 16 + k, device(x, y, zk, c)))
+            copies.append(remote(self.acc_2.at[zk], self.got_z.at[k], self.sems, 19 + k, device(x, y, zk, c)))
         return copies
 
     def third_start(self):
@@ -380,7 +413,7 @@
 def kernel(count, hidden, weight, partner, whitened, grad_weight, grad_hidden,
            tile, tile_got, tile_sems,
            cent, packed, summed, acc, got_c, got_1, acc_1, got_2, acc_2, got_z, full_z, sems_1, sems_2,
-           inv, inv_block, inv_row, white, grad, mirror, total, grad_z, grad_mean, late, high, low,
+           inv, inv_block, inv_row, white, grad, mirror, total, grad_z, grad_mean, late, hidden_t, high, low,
            strip, away, w_got_c, acc_a, acc_b, w_got_1, w_acc_1, w_got_2, w_acc_2, w_got_z, w_sems_1, w_sems_2):
     here = place()
     x, y, z, c = here
@@ -402,6 +435,7 @@
     sums = dot16(jnp.ones((8, N), bf16), hidden[...])
     for i in range(16):
         tile[0, 8 + i : 9 + i, :] = sums[0:1, i * BLK : (i + 1) * BLK]
+    hidden_t[...] = hidden[...].T
     pl.semaphore_wait(barrier, NZ * NC + NX * NY - 2)
     tile_sum(here, tile, tile_got, tile_sems)
     for i in range(8):
@@ -411,15 +445,16 @@
     split(cent[:N, :], high, low)
     reduce_buffers = (acc, got_c, got_1, acc_1, got_2, acc_2, got_z, full_z)
     row_buffers = (high, low, strip, away, w_got_c, acc_a, acc_b, w_got_1, w_acc_1, w_got_2, w_acc_2, w_got_z)
-    by_cent = RowScatter(here, hidden, *row_buffers, w_sems_1)
-    by_grad = RowScatter(here, hidden, *row_buffers, w_sems_2)
+    by_cent = RowScatter(here, hidden_t, *row_buffers, w_sems_1)
+    by_grad = RowScatter(here, hidden_t, *row_buffers, w_sems_2)
 
     def cent_strips():
         by_cent.strips()
         by_cent.core_start()
 
-    all_sum(here, packed, summed, *reduce_buffers, sems_1, {"first": cent_strips, "core back": by_cent.core_end}, {})
-    by_cent.first_start()
+    all_sum(here, packed, summed, *reduce_buffers, sems_1, {"first": cent_strips, "core back": by_cent.core_end})
+    by_cent.far_start()
+    by_cent.near_start()
 
     def to_second():
         by_cent.first_end()
@@ -429,7 +464,7 @@
         by_cent.second_end()
         by_cent.third_start()
 
-    inverse_factor(1.0 / (count - 1), summed, inv, inv_block, inv_row, {4: to_second, 6: to_third})
+    inverse_factor(1.0 / (count - 1), summed, inv, inv_block, inv_row, {2: by_cent.pass_on, 4: to_second, 6: to_third})
     by_cent.third_end(cent, N)
     for part in range(4):
         stop = part * 256 + 256
@@ -464,9 +499,17 @@
         )
     all_sum(
         here, packed, summed, *reduce_buffers, sems_2,
-        {"core": by_grad.strips, "first": by_grad.core_end},
-        {"core": by_grad.core_start, "first": by_grad.first_start},
+        {
+            "core": by_grad.strips,
+            "first": by_grad.core_start,
+            "second": by_grad.core_end,
+            "third": by_grad.far_start,
+            "third back": by_grad.near_start,
+            "core back": by_grad.pass_on,
+        },
     )
+    by_grad.first_end()
+    by_grad.second_start()
     lane1 = lax.broadcasted_iota(jnp.int32, (1, BLK), 1)
     r = lax.broadcasted_iota(jnp.int32, (BLK, BLK), 0)
     l = lax.broadcasted_iota(jnp.int32, (BLK, BLK), 1)
@@ -500,11 +543,9 @@
         grad_hidden[:, own] = dot16(grad_z[...], weight[own, :], 1, 1).astype(bf16)
         return carry
 
-    by_grad.first_end()
-    by_grad.second_start()
-    lax.fori_loop(0, 8, hidden_part, 0)
     by_grad.second_end()
     by_grad.third_start()
+    lax.fori_loop(0, 8, hidden_part, 0)
     units = jnp.broadcast_to(tile[2, pl.ds(8 + x * NY + y, 1), :], (8, BLK))
     mine = jnp.sum(jnp.where(lane == (z * NC + c) * 8 + sub, units, 0.0), axis=1, keepdims=True)
     by_grad.third_end(total, N)
@@ -533,11 +574,11 @@
             sem((2, 40)), sem((2, 40)),
             V((1024, 1024), f32), V((BLK, BLK), f32), V((BLK, 1024), f32), V((264, 1024), f32),
             V((256, 1024), f32), V((1024, 1024), f32), V((264, 1024), f32), V((256, 1024), bf16),
-            V((8, 1024), f32), V((8, 1024), f32), V((256, 1024), bf16), V((256, 1024), bf16),
+            V((8, 1024), f32), V((8, 1024), f32), V((2048, 256), bf16), V((256, 1024), bf16), V((256, 1024), bf16),
             V((8, 2, 8, 1024), f32), V((4, 4, 8, 8, 1024), f32), V((4, 4, 8, 8, 1024), f32),
-            V((4, 4, 8, 8, 512), f32), V((4, 4, 8, 8, 512), f32), V((2, 3, 4, 8, 8, 512), f32),
+            V((4, 4, 8, 8, 512), f32), V((4, 4, 8, 8, 512), f32), V((2, 6, 2, 8, 8, 512), f32),
             V((2, 4, 8, 8, 512), f32), V((2, 3, 8, 8, 512), f32), V((8, 2, 8, 512), f32), V((7, 2, 8, 512), f32),
-            sem((2, 23)), sem((2, 23)),
+            sem((2, 26)), sem((2, 26)),
         ],
         compiler_params=pltpu.CompilerParams(collective_id=0, has_side_effects=True, vmem_limit_bytes=60 * MB),
         name="whitening_step",

time: 246 us -> 219 us (0.89)
  Pallas kernels: 238 us -> 212 us
    pallas_call x1, Pallas kernels: 238 us -> 212 us  [body(): pl.pallas_call(functools.partial(kernel, count), out_shape=(jax.ShapeDtyp...]
where the time goes in v5:
time: 219 us; the launch traced here: 218 us
  Pallas kernels  212 us (97%)
  local copies, waits for them, and re-layouts  5.55 us (3%)
    pallas_call x1, Pallas kernels, body(): pl.pallas_call(functools.partial(kernel, count), out_shape=(jax.ShapeDtyp...  212 us
    unnamed x3, local copies, waits for them, and re-layouts  5.55 us

profile of v5, /device:TPU:0, one launch (start us, length us, event | category | flops | bytes accessed | tf_op | source)
XLA Modules:
  0.0 217.7 jit_solution(8507591640545444427)
XLA Ops:
  0.6 211.5 %whitening_step.1 = (bf16[256,1024]{1,0:T(8,128)(2,1)}, f32[8,1024]{1,0:T(8,128)}, bf16[256,2048]{1,0:T(8,128)(2,1)}) custom-call(bf16[256,2048]{1,0:T(8,128)(2,1)} %hidden.1, bf16[2048,1024]{1,0:T(8,128)(2,1)} %weight.1, s32[1,256]{1,0:T(1,128)} %partner.1), custom_call_target="tpu_custom_call" | custom-call | tf_op jit(solution)/shard_map/whitening_step/pallas_call | solution.py:560
  212.2 1.9 copy.9
  214.0 1.4 copy.10
  215.4 2.3 %copy.11 = bf16[256,2048]{1,0:T(8,128)(2,1)} copy(bf16[256,2048]{1,0:T(8,128)(2,1)} %get-tuple-element.8) | data formatting | bytes 2097152

commit v6 on v5

--- a/solution.py
+++ b/solution.py
@@ -129,7 +129,24 @@
     return [jnp.where(lane <= sub + 8 * p, pan[p], 0.0) for p in range(16)]
 
 
-def inverse_factor(scale, in_ref, out_ref, inv_ref, row_ref, beside):
+def thirds(v):
+    high = v.astype(bf16)
+    rest = v - high.astype(f32)
+    mid = rest.astype(bf16)
+    return high, mid, (rest - mid.astype(f32)).astype(bf16)
+
+
+def left_stack(v):
+    h, m, l = thirds(v)
+    return jnp.concatenate([h, h, m, h, l, m], axis=1)
+
+
+def right_stack(v, axis):
+    h, m, l = thirds(v)
+    return jnp.concatenate([h, m, h, l, h, m], axis=axis)
+
+
+def inverse_factor(scale, in_ref, out_ref, inv_ref, stack_ref, beside):
     for i in range(8):
         for j in range(i + 1):
             block = get_block(in_ref, i, j) * scale
@@ -142,31 +159,48 @@
             else:
                 out_ref[rows, cols] = block
                 out_ref[cols, rows] = turned
+    out_ref[1024:, :] = jnp.zeros((7 * BLK, 1024), f32)
     lane = lax.broadcasted_iota(jnp.int32, (BLK, 1024), 1)
+
+    def factor(block):
+        return inverse_factor_block([block[8 * p : 8 * p + 8, :] for p in range(16)])
+
+    def keep(tiles):
+        for p, tile in enumerate(tiles):
+            inv_ref[8 * p : 8 * p + 8, :] = tile
+
+    def scaled_row(i):
+        own = span(i * BLK, BLK)
+        inv = inv_ref[...]
+        row = dot16(left_stack(inv), right_stack(out_ref[own, :], 0))
+        inside = (lane >= i * BLK) & (lane < (i + 1) * BLK)
+        row = jnp.where(inside, jnp.concatenate([inv] * 8, axis=1), row)
+        out_ref[own, :] = jnp.where(lane < (i + 1) * BLK, row, 0.0)
+        return row
+
+    keep(factor(out_ref[0:BLK, 0:BLK]))
 
     def step(i, carry):
         for at, work in beside.items():
             pl.when(i == at)(work)
-        own = span(i * BLK, BLK)
-        pans = [out_ref[span(i * BLK + 8 * p, 8), own] for p in range(16)]
-        for p, tile in enumerate(inverse_factor_block(pans)):
-            inv_ref[8 * p : 8 * p + 8, :] = tile
+        own, nxt = span(i * BLK, BLK), span((i + 1) * BLK, BLK)
+        below = pl.ds(pl.multiple_of((i + 1) * BLK, BLK), 7 * BLK)
         inv = inv_ref[...]
-        row_ref[...] = dots(inv, out_ref[own, :])
-        row_ref[:, own] = inv
-        out_ref[own, :] = jnp.where(lane < (i + 1) * BLK, row_ref[...], 0.0)
-
-        def lower(j, inner):
-            its = span(j * BLK, BLK)
-            left = dots(out_ref[its, own], inv_ref[...], 1, 1)
-            out_ref[its, own] = jnp.zeros((BLK, BLK), f32)
-            out_ref[its, :] = out_ref[its, :] - dots(left, row_ref[...])
-            return inner
-
-        lax.fori_loop(i + 1, 8, lower, 0)
+        left = dots(out_ref[nxt, own], inv, 1, 1)
+        block = out_ref[nxt, nxt] - dots(left, left, 1, 1)
+        tiles = factor(block)
+        stack_ref[...] = right_stack(scaled_row(i), 0)
+        left = dot16(left_stack(out_ref[below, own]), right_stack(inv, 1), 1, 1)
+        out_ref[below, own] = jnp.zeros((7 * BLK, BLK), f32)
+        left = left_stack(left)
+        for part in range(4):
+            cols = slice(part * 256, part * 256 + 256)
+            out_ref[below, cols] = out_ref[below, cols] - dot16(left, stack_ref[:, cols])
+        keep(tiles)
         return carry
 
-    lax.fori_loop(0, 8, step, 0)
+    lax.fori_loop(0, 7, step, 0)
+    scaled_row(7)
 
 
 def get_block(ref, i, j):
@@ -413,7 +447,7 @@
 def kernel(count, hidden, weight, partner, whitened, grad_weight, grad_hidden,
            tile, tile_got, tile_sems,
            cent, packed, summed, acc, got_c, got_1, acc_1, got_2, acc_2, got_z, full_z, sems_1, sems_2,
-           inv, inv_block, inv_row, white, grad, mirror, total, grad_z, grad_mean, late, hidden_t, high, low,
+           inv, inv_block, inv_stack, white, grad, mirror, total, grad_z, grad_mean, late, hidden_t, high, low,
            strip, away, w_got_c, acc_a, acc_b, w_got_1, w_acc_1, w_got_2, w_acc_2, w_got_z, w_sems_1, w_sems_2):
     here = place()
     x, y, z, c = here
@@ -464,7 +498,7 @@
         by_cent.second_end()
         by_cent.third_start()
 
-    inverse_factor(1.0 / (count - 1), summed, inv, inv_block, inv_row, {2: by_cent.pass_on, 4: to_second, 6: to_third})
+    inverse_factor(1.0 / (count - 1), summed, inv, inv_block, inv_stack, {2: by_cent.pass_on, 4: to_second, 6: to_third})
     by_cent.third_end(cent, N)
     for part in range(4):
         stop = part * 256 + 256
@@ -534,7 +568,7 @@
     for part in range(4):
         start_at = part * 256
         cols = slice(start_at, start_at + 256)
-        both = dots(total[:, start_at:], inv[start_at:, cols])
+        both = dots(total[:, start_at:], inv[start_at:1024, cols])
         grad_z[:, cols] = both[:N].astype(bf16)
         late[:, cols] = both[N:]
 
@@ -550,7 +584,7 @@
     mine = jnp.sum(jnp.where(lane == (z * NC + c) * 8 + sub, units, 0.0), axis=1, keepdims=True)
     by_grad.third_end(total, N)
     rows = total[N:, :] - mine * grad_mean[...]
-    grad_weight[...] = late[...] + dots(rows, inv[...])
+    grad_weight[...] = late[...] + dots(rows, inv[:1024, :])
 
 
 def body(hidden, weight, partners):
@@ -572,7 +606,7 @@
             V((288, 8, 128), f32), V((288, 8, 128), f32), V((2, 3, 36, 8, 128), f32), V((2, 36, 8, 128), f32),
             V((2, 3, T, 8, 128), f32), V((24, 8, 128), f32), V((7, 3, 8, 128), f32), V((24, 8, 128), f32),
             sem((2, 40)), sem((2, 40)),
-            V((1024, 1024), f32), V((BLK, BLK), f32), V((BLK, 1024), f32), V((264, 1024), f32),
+            V((1920, 1024), f32), V((BLK, BLK), f32), V((768, 1024), bf16), V((264, 1024), f32),
             V((256, 1024), f32), V((1024, 1024), f32), V((264, 1024), f32), V((256, 1024), bf16),
             V((8, 1024), f32), V((8, 1024), f32), V((2048, 256), bf16), V((256, 1024), bf16), V((256, 1024), bf16),
             V((8, 2, 8, 1024), f32), V((4, 4, 8, 8, 1024), f32), V((4, 4, 8, 8, 1024), f32),

time: 219 us -> 199 us (0.909)
  Pallas kernels: 212 us -> 191 us
    pallas_call x1, Pallas kernels: 212 us -> 191 us  [body(): pl.pallas_call(functools.partial(kernel, count), out_shape=(jax.ShapeDtyp...]
where the time goes in v6:
time: 199 us; the launch traced here: 197 us
  Pallas kernels  191 us (96%)
  local copies, waits for them, and re-layouts  5.55 us (3%)
    pallas_call x1, Pallas kernels, body(): pl.pallas_call(functools.partial(kernel, count), out_shape=(jax.ShapeDtyp...  191 us
    unnamed x3, local copies, waits for them, and re-layouts  5.55 us

profile of v6, /device:TPU:0, one launch (start us, length us, event | category | flops | bytes accessed | tf_op | source)
XLA Modules:
  0.0 197.3 jit_solution(16712143539110871335)
XLA Ops:
  0.6 191.2 %whitening_step.1 = (bf16[256,1024]{1,0:T(8,128)(2,1)}, f32[8,1024]{1,0:T(8,128)}, bf16[256,2048]{1,0:T(8,128)(2,1)}) custom-call(bf16[256,2048]{1,0:T(8,128)(2,1)} %hidden.1, bf16[2048,1024]{1,0:T(8,128)(2,1)} %weight.1, s32[1,256]{1,0:T(1,128)} %partner.1), custom_call_target="tpu_custom_call" | custom-call | tf_op jit(solution)/shard_map/whitening_step/pallas_call | solution.py:594
  191.8 1.9 copy.9
  193.7 1.4 copy.10
  195.0 2.3 %copy.11 = bf16[256,2048]{1,0:T(8,128)(2,1)} copy(bf16[256,2048]{1,0:T(8,128)(2,1)} %get-tuple-element.8) | data formatting | bytes 2097152

commit v7 on v6

--- a/solution.py
+++ b/solution.py
@@ -299,11 +299,17 @@
     for k in range(3):
         copies.append(send(first, first, sems, 33 + k, xs[k]))
         copies.append(send(second, second, sems, 36 + k, ys[k]))
-    wait(copies)
-    first = out_ref.at[pl.ds(base, 288)]
-    copy = send(first, first, sems, 39, across)
+    over = [send(first, first, sems, 39, across), send(second, second, sems, 40, across)]
+    during.get("first back", nothing)()
+    for k in range(3):
+        copies[2 * k].wait()
+        chunk = out_ref.at[pl.ds(base + x_at[2 - k] * 36, 36)]
+        over.append(send(chunk, chunk, sems, 41 + 2 * k, across))
+        copies[2 * k + 1].wait()
+        chunk = out_ref.at[pl.ds(base + 144 + y_at[2 - k] * 36, 36)]
+        over.append(send(chunk, chunk, sems, 42 + 2 * k, across))
     during.get("core back", nothing)()
-    copy.wait()
+    wait(over)
 
 
 class RowScatter:
@@ -444,14 +450,19 @@
     low[...] = (rows - high[...].astype(f32)).astype(bf16)
 
 
-def kernel(count, hidden, weight, partner, whitened, grad_weight, grad_hidden,
-           tile, tile_got, tile_sems,
+def kernel(count, hidden_in, weight_in, partner, whitened, grad_weight, grad_hidden,
+           hidden, weight, in_sems, tile, tile_got, tile_sems,
            cent, packed, summed, acc, got_c, got_1, acc_1, got_2, acc_2, got_z, full_z, sems_1, sems_2,
            inv, inv_block, inv_stack, white, grad, mirror, total, grad_z, grad_mean, late, hidden_t, high, low,
            strip, away, w_got_c, acc_a, acc_b, w_got_1, w_acc_1, w_got_2, w_acc_2, w_got_z, w_sems_1, w_sems_2):
     here = place()
     x, y, z, c = here
     N = 256
+    loads = [
+        pltpu.make_async_copy(hidden_in, hidden, in_sems.at[0]),
+        pltpu.make_async_copy(weight_in, weight, in_sems.at[1]),
+    ]
+    start(loads)
     barrier = pltpu.get_barrier_semaphore()
     for k in range(1, NZ * NC):
         own = lax.rem(z * NC + c + k, NZ * NC)
@@ -459,6 +470,9 @@
     for k in range(1, NX * NY):
         own = lax.rem(x * NY + y + k, NX * NY)
         pl.semaphore_signal(barrier, inc=1, device_id=device(lax.div(own, NY), lax.rem(own, NY), z, c), device_id_type=MESH)
+    loads[0].wait()
+    hidden_t[...] = hidden[...].T
+    loads[1].wait()
     for part in range(4):
         cols = slice(part * 256, part * 256 + 256)
         strip_e = dot16(hidden[...], weight[:, cols])
@@ -469,7 +483,6 @@
     sums = dot16(jnp.ones((8, N), bf16), hidden[...])
     for i in range(16):
         tile[0, 8 + i : 9 + i, :] = sums[0:1, i * BLK : (i + 1) * BLK]
-    hidden_t[...] = hidden[...].T
     pl.semaphore_wait(barrier, NZ * NC + NX * NY - 2)
     tile_sum(here, tile, tile_got, tile_sems)
     for i in range(8):
@@ -531,6 +544,10 @@
         packed[at] = jnp.where(
             (lane >= 64) & (sub == 0), swapped, jnp.where((lane >= 64) & (sub == 1), own, packed[at])
         )
+    def to_second_grad():
+        by_grad.first_end()
+        by_grad.second_start()
+
     all_sum(
         here, packed, summed, *reduce_buffers, sems_2,
         {
@@ -539,11 +556,10 @@
             "second": by_grad.core_end,
             "third": by_grad.far_start,
             "third back": by_grad.near_start,
-            "core back": by_grad.pass_on,
+            "first back": by_grad.pass_on,
+            "core back": to_second_grad,
         },
     )
-    by_grad.first_end()
-    by_grad.second_start()
     lane1 = lax.broadcasted_iota(jnp.int32, (1, BLK), 1)
     r = lax.broadcasted_iota(jnp.int32, (BLK, BLK), 0)
     l = lax.broadcasted_iota(jnp.int32, (BLK, BLK), 1)
@@ -565,6 +581,8 @@
     for part in range(4):
         cols = slice(part * 256, part * 256 + 256)
         total[:, cols] = total[:, cols] - dots(white[...], mirror[:, cols])
+    by_grad.second_end()
+    by_grad.third_start()
     for part in range(4):
         start_at = part * 256
         cols = slice(start_at, start_at + 256)
@@ -577,8 +595,6 @@
         grad_hidden[:, own] = dot16(grad_z[...], weight[own, :], 1, 1).astype(bf16)
         return carry
 
-    by_grad.second_end()
-    by_grad.third_start()
     lax.fori_loop(0, 8, hidden_part, 0)
     units = jnp.broadcast_to(tile[2, pl.ds(8 + x * NY + y, 1), :], (8, BLK))
     mine = jnp.sum(jnp.where(lane == (z * NC + c) * 8 + sub, units, 0.0), axis=1, keepdims=True)
@@ -598,14 +614,15 @@
             jax.ShapeDtypeStruct((8, 1024), f32),
             jax.ShapeDtypeStruct((256, 2048), bf16),
         ),
-        in_specs=[vmem] * 3,
+        in_specs=[pl.BlockSpec(memory_space=pl.ANY)] * 2 + [vmem],
         out_specs=(vmem,) * 3,
         scratch_shapes=[
+            V((256, 2048), bf16), V((2048, 1024), bf16), sem((2,)),
             V((3, 24, 128), f32), V((2, 15, 24, 128), f32), sem((2, 30)),
             V((264, 1024), f32), V((576, 8, 128), f32), V((576, 8, 128), f32),
             V((288, 8, 128), f32), V((288, 8, 128), f32), V((2, 3, 36, 8, 128), f32), V((2, 36, 8, 128), f32),
             V((2, 3, T, 8, 128), f32), V((24, 8, 128), f32), V((7, 3, 8, 128), f32), V((24, 8, 128), f32),
-            sem((2, 40)), sem((2, 40)),
+            sem((2, 47)), sem((2, 47)),
             V((1920, 1024), f32), V((BLK, BLK), f32), V((768, 1024), bf16), V((264, 1024), f32),
             V((256, 1024), f32), V((1024, 1024), f32), V((264, 1024), f32), V((256, 1024), bf16),
             V((8, 1024), f32), V((8, 1024), f32), V((2048, 256), bf16), V((256, 1024), bf16), V((256, 1024), bf16),

time: 199 us -> 196 us (0.985)
  Pallas kernels: 191 us -> 187 us
    pallas_call x1, Pallas kernels: 191 us -> 187 us  [body(): pl.pallas_call(functools.partial(kernel, count), out_shape=(jax.ShapeDtyp...]
where the time goes in v7:
time: 196 us; the launch traced here: 194 us
  Pallas kernels  187 us (95%)
  local copies, waits for them, and re-layouts  5.55 us (3%)
    pallas_call x1, Pallas kernels, body(): pl.pallas_call(functools.partial(kernel, count), out_shape=(jax.ShapeDtyp...  187 us
    unnamed x3, local copies, waits for them, and re-layouts  5.55 us

profile of v7, /device:TPU:0, one launch (start us, length us, event | category | flops | bytes accessed | tf_op | source)
XLA Modules:
  0.0 193.6 jit_solution(727066087522464679)
XLA Ops:
  0.6 187.4 %whitening_step.1 = (bf16[256,1024]{1,0:T(8,128)(2,1)}, f32[8,1024]{1,0:T(8,128)}, bf16[256,2048]{1,0:T(8,128)(2,1)}) custom-call(bf16[256,2048]{1,0:T(8,128)(2,1)} %hidden_in.1, bf16[2048,1024]{1,0:T(8,128)(2,1)} %weight_in.1, s32[1,256]{1,0:T(1,128)} %partner.1), custom_call_target="tpu_custom_call" | custom-call | tf_op jit(solution)/shard_map/whitening_step/pallas_call | solution.py:610
  188.0 1.9 copy.9
  189.9 1.4 copy.10
  191.3 2.3 %copy.11 = bf16[256,2048]{1,0:T(8,128)(2,1)} copy(bf16[256,2048]{1,0:T(8,128)(2,1)} %get-tuple-element.8) | data formatting | bytes 2097152

commit v8 on v7

--- a/solution.py
+++ b/solution.py
@@ -603,11 +603,35 @@
     grad_weight[...] = late[...] + dots(rows, inv[:1024, :])
 
 
+def hand_over_kernel(whitened, grad_weight, grad_hidden, whitened_out, grad_weight_out, grad_hidden_out, sems):
+    copies = [pltpu.make_async_copy(grad_weight, grad_weight_out, sems.at[0])]
+    for k in range(2):
+        rows = pl.ds(k * 128, 128)
+        copies.append(pltpu.make_async_copy(whitened.at[rows], whitened_out.at[rows], sems.at[1 + k]))
+    for k in range(4):
+        rows = pl.ds(k * 64, 64)
+        copies.append(pltpu.make_async_copy(grad_hidden.at[rows], grad_hidden_out.at[rows], sems.at[3 + k]))
+    start(copies)
+    wait(copies)
+
+
+def hand_over(results):
+    anywhere = pl.BlockSpec(memory_space=pl.ANY)
+    return pl.pallas_call(
+        hand_over_kernel,
+        out_shape=tuple(jax.ShapeDtypeStruct(a.shape, a.dtype) for a in results),
+        in_specs=[anywhere] * 3,
+        out_specs=(anywhere,) * 3,
+        scratch_shapes=[pltpu.SemaphoreType.DMA((7,))],
+        name="hand_over",
+    )(*results)
+
+
 def body(hidden, weight, partners):
     count = hidden.shape[0] * lax.axis_size("group") * lax.axis_size("dp")
     vmem = pl.BlockSpec(memory_space=pltpu.VMEM)
     V, sem = pltpu.VMEM, pltpu.SemaphoreType.DMA
-    return pl.pallas_call(
+    results = pl.pallas_call(
         functools.partial(kernel, count),
         out_shape=(
             jax.ShapeDtypeStruct((256, 1024), bf16),
@@ -634,6 +658,7 @@
         compiler_params=pltpu.CompilerParams(collective_id=0, has_side_effects=True, vmem_limit_bytes=60 * MB),
         name="whitening_step",
     )(hidden, weight, partners)
+    return hand_over(results)
 
 
 def solution(mesh):

time: 196 us -> 240 us (1.22)
  Pallas kernels: 187 us -> 237 us
  local copies, waits for them, and re-layouts: 5.55 us -> 0 us
    pallas_call x0 -> x1, Pallas kernels: none -> 49.8 us  [hand_over(): pl.pallas_call(hand_over_kernel, out_shape=tuple((jax.ShapeDtypeStruct(a....]
    unnamed x3 -> x0, local copies, waits for them, and re-layouts: 5.55 us -> none
where the time goes in v8:
time: 240 us; the launch traced here: 238 us
  Pallas kernels  237 us (99%)
    pallas_call x1, Pallas kernels, body(): pl.pallas_call(functools.partial(kernel, count), out_shape=(jax.ShapeDtyp...  187 us
    pallas_call x1, Pallas kernels, hand_over(): pl.pallas_call(hand_over_kernel, out_shape=tuple((jax.ShapeDtypeStruct(a....  49.8 us

profile of v8, /device:TPU:0, one launch (start us, length us, event | category | flops | bytes accessed | tf_op | source)
XLA Modules:
  0.0 238.0 jit_solution(11093313270654763976)
XLA Ops:
  0.6 187.4 %whitening_step.1 = (bf16[256,1024]{1,0:T(8,128)(2,1)}, f32[8,1024]{1,0:T(8,128)}, bf16[256,2048]{1,0:T(8,128)(2,1)}) custom-call(bf16[256,2048]{1,0:T(8,128)(2,1)} %hidden_in.1, bf16[2048,1024]{1,0:T(8,128)(2,1)} %weight_in.1, s32[1,256]{1,0:T(1,128)} %partner.1), custom_call_target="tpu_custom_call" | custom-call | tf_op jit(solution)/shard_map/whitening_step/pallas_call | solution.py:634
  188.0 49.8 %hand_over.1 = (bf16[256,1024]{1,0:T(8,128)(2,1)}, f32[8,1024]{1,0:T(8,128)}, bf16[256,2048]{1,0:T(8,128)(2,1)}) custom-call(bf16[256,1024]{1,0:T(8,128)(2,1)} %get-tuple-element.6.whitened, f32[8,1024]{1,0:T(8,128)} %get-tuple-element.7.grad_weight, bf16[256,2048]{1,0:T(8,128)(2,1)} %get-tuple-element.8.grad_hidden), custom_call_target="tpu_custom_call" | custom-call | tf_op jit(solution)/shard_map/hand_over/pallas_call | solution.py:620
